TPU v7x, 32 devices: a whole 2x2x4 slice. The times are simulated.
32 devices in a mesh: dp: 8 (over z, y), tensor: 4 (over x, core).
Axes of the slice: x: 2, y: 2, z: 4, core: 2. Of those that a mesh axis runs over, the one named last changes fastest.
Arguments:
- tokens: bfloat16 [16384, 1280], P(('dp', 'tensor')), may hold values from -6 to 6
- cotangent: bfloat16 [16384, 1280], P(('dp', 'tensor')), may hold values from -6 to 6
- block_ids: int32 [8, 2048], P('dp'), may hold values from 0 to 15, never falling along the last dimension, each value on 1 to 256 neighbouring positions
- attn_gain: float32 [1280], replicated, may hold values from 0.5 to 1.5
- w_query: bfloat16 [1280, 1280], P('dp', 'tensor'), may hold values from -0.15625 to 0.15625
- w_key: bfloat16 [1280, 1280], P('dp', 'tensor'), may hold values from -0.15625 to 0.15625
- w_value: bfloat16 [1280, 1280], P('dp', 'tensor'), may hold values from -0.15625 to 0.15625
- query_scale: float32 [80], replicated, may hold values from 0.5 to 2.5
- w_out: bfloat16 [1280, 1280], P('tensor', 'dp'), may hold values from -0.5 to 0.5
- mlp_gain: float32 [1280], replicated, may hold values from 0.5 to 1.5
- w_up: bfloat16 [1280, 1280], P('dp', 'tensor'), may hold values from -0.15625 to 0.15625
- b_up: float32 [1280], replicated, may hold values from -3 to 3
- w_down: bfloat16 [1280, 1280], P('tensor', 'dp'), may hold values from -0.25 to 0.25
- b_down: float32 [1280], replicated, may hold values from -3 to 3
Outputs:
- output: bfloat16 [16384, 1280], P(('dp', 'tensor'))
- d_tokens: bfloat16 [16384, 1280], P(('dp', 'tensor'))
- d_attn_gain: float32 [1280], replicated
- d_w_query: float32 [1280, 1280], P('dp', 'tensor')
- d_w_key: float32 [1280, 1280], P('dp', 'tensor')
- d_w_value: float32 [1280, 1280], P('dp', 'tensor')
- d_query_scale: float32 [80], replicated
- d_w_out: float32 [1280, 1280], P('tensor', 'dp')
- d_mlp_gain: float32 [1280], replicated
- d_w_up: float32 [1280, 1280], P('dp', 'tensor')
- d_b_up: float32 [1280], replicated
- d_w_down: float32 [1280, 1280], P('tensor', 'dp')
- d_b_down: float32 [1280], replicated
Inputs may be any that keep to these rules, and one draw needn't show every extreme that they name: `block_ids`: in each sequence the block numbers never fall along positions, each number from 0 to 15 appears, a block spans 1 to 256 positions, and one block spans exactly 256.
All inputs are finite; a program needn't handle non-finite values.
Results may differ from a plain program's by a relative error of at most 0.014.
The roundings to bfloat16 on the way count: a program that leaves them out, or rounds other values in their place, can miss the bound.
Values may be sent and summed in bfloat16 or wider, within the bound.
A program may use at most 192 MiB of HBM per device.

v0:
```python
import math

import jax
import jax.numpy as jnp
from jax import lax
from jax.sharding import PartitionSpec as P

HD = 80


EPSILON = 1e-06
SCORE_BASE = 1.442695041
MASKED = -1e30


def rms_stats(values_in):
    inverse = lax.rsqrt(jnp.mean(values_in * values_in, axis=-1, keepdims=True) + EPSILON)
    return (values_in * inverse, inverse)


def rms_back(grad_in, normed, inverse, gain):
    scaled = grad_in * gain
    back_grad = inverse * (scaled - normed * jnp.mean(scaled * normed, axis=-1, keepdims=True))
    return (back_grad, jnp.sum(grad_in * normed, axis=0))


def block_scores(query_block, query_ids, key_all, key_ids):
    scores = jnp.einsum("qhd,khd->hqk", query_block, key_all, preferred_element_type=jnp.float32)
    visible = query_ids[:, None] >= key_ids[None, :]
    return jnp.where(visible[None], scores, MASKED)


def attention_forward(queries, key_all, value_all, key_ids, block_rows):
    length, heads, depth = queries.shape
    count_blocks = length // block_rows

    def one_block(block_pair):
        query_block, query_ids = block_pair
        scores = block_scores(query_block, query_ids, key_all, key_ids)
        highest = jnp.max(scores, axis=-1, keepdims=True)
        weights = jnp.exp(scores - highest)
        summed = jnp.sum(weights, axis=-1, keepdims=True)
        probs = (weights / summed).astype(jnp.bfloat16)
        attended = jnp.einsum("hqk,khd->qhd", probs, value_all, preferred_element_type=jnp.float32)
        return (attended.astype(jnp.bfloat16), highest + jnp.log(summed))

    attended, log_sums = lax.map(
        one_block,
        (
            queries.reshape(count_blocks, block_rows, heads, depth),
            key_ids.reshape(count_blocks, block_rows),
        ),
    )
    return (attended.reshape(length, heads, depth), log_sums)


def attention_backward(queries, key_all, value_all, key_ids, log_sums, grad_attended, block_rows):
    length, heads, depth = queries.shape
    count_blocks = length // block_rows

    def one_block(carried, block_items):
        key_grads, value_grads = carried
        query_block, query_ids, block_lse, grad_block = block_items
        scores = block_scores(query_block, query_ids, key_all, key_ids)
        probs = jnp.exp(scores - block_lse)
        value_grads = value_grads + jnp.einsum(
            "hqk,qhd->khd",
            probs.astype(jnp.bfloat16),
            grad_block,
            preferred_element_type=jnp.float32,
        )
        grad_probs = jnp.einsum(
            "qhd,khd->hqk", grad_block, value_all, preferred_element_type=jnp.float32
        )
        inner = jnp.sum(probs * grad_probs, axis=-1, keepdims=True)
        grad_scores = (probs * (grad_probs - inner)).astype(jnp.bfloat16)
        query_grads = jnp.einsum(
            "hqk,khd->qhd", grad_scores, key_all, preferred_element_type=jnp.float32
        )
        key_grads = key_grads + jnp.einsum(
            "hqk,qhd->khd", grad_scores, query_block, preferred_element_type=jnp.float32
        )
        return ((key_grads, value_grads), query_grads)

    empty = jnp.zeros((length, heads, depth), jnp.float32)
    (key_grads, value_grads), query_grads = lax.scan(
        one_block,
        (empty, empty),
        (
            queries.reshape(count_blocks, block_rows, heads, depth),
            key_ids.reshape(count_blocks, block_rows),
            log_sums,
            grad_attended.reshape(count_blocks, block_rows, heads, depth),
        ),
    )
    return (query_grads.reshape(length, heads, depth), key_grads, value_grads)


def body(
    tokens,
    cotangent,
    block_ids,
    attn_gain,
    w_query,
    w_key,
    w_value,
    query_scale,
    w_out,
    mlp_gain,
    w_up,
    b_up,
    w_down,
    b_down,
):
    gathered = (
        lax.all_gather(w_query, "dp", axis=0, tiled=True),
        lax.all_gather(w_key, "dp", axis=0, tiled=True),
        lax.all_gather(w_value, "dp", axis=0, tiled=True),
        lax.all_gather(w_out, "dp", axis=1, tiled=True),
        lax.all_gather(w_up, "dp", axis=0, tiled=True),
        lax.all_gather(w_down, "dp", axis=1, tiled=True),
    )
    full_query, full_key, full_value, full_out, full_up, full_down = gathered
    local_heads = full_query.shape[1] // HD
    seq_ids = block_ids[0]
    length = seq_ids.shape[0]
    block_rows = min(512, length)
    tokens_f32 = tokens.astype(jnp.float32)
    cot_f32 = cotangent.astype(jnp.float32)
    normed_one, inverse_one = rms_stats(tokens_f32)
    normed_all = lax.all_gather(
        (normed_one * attn_gain).astype(jnp.bfloat16), "tensor", axis=0, tiled=True
    )
    softplus_scale = jnp.log1p(jnp.exp(query_scale))
    factor = SCORE_BASE / math.sqrt(HD) * softplus_scale
    query_f32 = jnp.dot(normed_all, full_query, preferred_element_type=jnp.float32).reshape(
        length, local_heads, HD
    )
    queries = (query_f32 * factor).astype(jnp.bfloat16)
    key_all = (
        jnp.dot(normed_all, full_key, preferred_element_type=jnp.float32)
        .astype(jnp.bfloat16)
        .reshape(length, local_heads, HD)
    )
    value_all = (
        jnp.dot(normed_all, full_value, preferred_element_type=jnp.float32)
        .astype(jnp.bfloat16)
        .reshape(length, local_heads, HD)
    )
    attended, log_sums = attention_forward(queries, key_all, value_all, seq_ids, block_rows)
    attended_flat = attended.reshape(length, local_heads * HD)
    hidden_state = tokens_f32 + lax.psum_scatter(
        jnp.dot(attended_flat, full_out, preferred_element_type=jnp.float32),
        "tensor",
        scatter_dimension=0,
        tiled=True,
    )
    normed_two, inverse_two = rms_stats(hidden_state)
    normed_mlp_local = (normed_two * mlp_gain).astype(jnp.bfloat16)
    wide_up, wide_down = (
        lax.all_gather(full_up, "tensor", axis=1, tiled=True),
        lax.all_gather(full_down, "tensor", axis=0, tiled=True),
    )
    pre_act = jnp.dot(normed_mlp_local, wide_up, preferred_element_type=jnp.float32) + b_up
    sigmoid_pre = jax.nn.sigmoid(pre_act)
    activation = (pre_act * sigmoid_pre).astype(jnp.bfloat16)
    result = (
        hidden_state + jnp.dot(activation, wide_down, preferred_element_type=jnp.float32) + b_down
    )
    output = result.astype(jnp.bfloat16)
    back_query, back_key, back_value, back_out, back_up, back_down = (
        lax.all_gather(w_query, "dp", axis=0, tiled=True),
        lax.all_gather(w_key, "dp", axis=0, tiled=True),
        lax.all_gather(w_value, "dp", axis=0, tiled=True),
        lax.all_gather(w_out, "dp", axis=1, tiled=True),
        lax.all_gather(w_up, "dp", axis=0, tiled=True),
        lax.all_gather(w_down, "dp", axis=1, tiled=True),
    )
    grad_down_wide = jnp.einsum(
        "gf,gd->fd", activation, cotangent, preferred_element_type=jnp.float32
    )
    grad_act = jnp.einsum("gd,fd->gf", cotangent, wide_down, preferred_element_type=jnp.float32)
    grad_pre = (grad_act * sigmoid_pre * (1.0 + pre_act * (1.0 - sigmoid_pre))).astype(jnp.bfloat16)
    bias_full = jnp.sum(grad_pre, axis=0, dtype=jnp.float32)
    grad_up_wide = jnp.einsum(
        "gd,gf->df", normed_mlp_local, grad_pre, preferred_element_type=jnp.float32
    )
    grad_normed_two = jnp.einsum("gf,df->gd", grad_pre, wide_up, preferred_element_type=jnp.float32)
    grad_up, grad_down = (
        lax.psum_scatter(grad_up_wide, "tensor", scatter_dimension=1, tiled=True),
        lax.psum_scatter(grad_down_wide, "tensor", scatter_dimension=0, tiled=True),
    )
    from_mlp, grad_mlp_gain = rms_back(grad_normed_two, normed_two, inverse_two, mlp_gain)
    grad_hidden = cot_f32 + from_mlp
    branch_all = lax.all_gather(grad_hidden.astype(jnp.bfloat16), "tensor", axis=0, tiled=True)
    grad_out = jnp.einsum(
        "gc,gd->cd", attended_flat, branch_all, preferred_element_type=jnp.float32
    )
    grad_attended = jnp.einsum(
        "gd,cd->gc", branch_all, back_out, preferred_element_type=jnp.float32
    ).astype(jnp.bfloat16)
    grad_attended = grad_attended.reshape(length, local_heads, HD)
    grad_scaled, grad_keys, grad_values = attention_backward(
        queries, key_all, value_all, seq_ids, log_sums, grad_attended, block_rows
    )
    grad_scale = (
        jnp.sum(grad_scaled * query_f32, axis=(0, 1))
        * (SCORE_BASE / math.sqrt(HD))
        * jax.nn.sigmoid(query_scale)
    )
    grad_query_rows = (grad_scaled * factor).astype(jnp.bfloat16).reshape(length, local_heads * HD)
    grad_key_rows = grad_keys.astype(jnp.bfloat16).reshape(length, local_heads * HD)
    grad_value_rows = grad_values.astype(jnp.bfloat16).reshape(length, local_heads * HD)
    grad_query = jnp.einsum(
        "gd,gc->dc", normed_all, grad_query_rows, preferred_element_type=jnp.float32
    )
    grad_key = jnp.einsum(
        "gd,gc->dc", normed_all, grad_key_rows, preferred_element_type=jnp.float32
    )
    grad_value = jnp.einsum(
        "gd,gc->dc", normed_all, grad_value_rows, preferred_element_type=jnp.float32
    )
    total_grad = jnp.einsum(
        "gc,dc->gd", grad_query_rows, back_query, preferred_element_type=jnp.float32
    )
    total_grad = total_grad + jnp.einsum(
        "gc,dc->gd", grad_key_rows, back_key, preferred_element_type=jnp.float32
    )
    grad_normed_one = lax.psum_scatter(
        total_grad
        + jnp.einsum("gc,dc->gd", grad_value_rows, back_value, preferred_element_type=jnp.float32),
        "tensor",
        scatter_dimension=0,
        tiled=True,
    )
    from_attn, grad_attn_gain = rms_back(grad_normed_one, normed_one, inverse_one, attn_gain)
    grad_tokens = (grad_hidden + from_attn).astype(jnp.bfloat16)
    shard_query, shard_key, shard_value, shard_out, shard_up, shard_down = (
        lax.psum_scatter(grad_query, "dp", scatter_dimension=0, tiled=True),
        lax.psum_scatter(grad_key, "dp", scatter_dimension=0, tiled=True),
        lax.psum_scatter(grad_value, "dp", scatter_dimension=0, tiled=True),
        lax.psum_scatter(grad_out, "dp", scatter_dimension=1, tiled=True),
        lax.psum_scatter(grad_up, "dp", scatter_dimension=0, tiled=True),
        lax.psum_scatter(grad_down, "dp", scatter_dimension=1, tiled=True),
    )
    sum_attn_gain, sum_scale, sum_mlp_gain, sum_bias_up, sum_bias_down = lax.psum(
        (grad_attn_gain, grad_scale, grad_mlp_gain, bias_full, jnp.sum(cot_f32, axis=0)),
        ("dp", "tensor"),
    )
    return (
        output,
        grad_tokens,
        sum_attn_gain,
        shard_query,
        shard_key,
        shard_value,
        sum_scale,
        shard_out,
        sum_mlp_gain,
        shard_up,
        sum_bias_up,
        shard_down,
        sum_bias_down,
    )


def solution(mesh):
    placed = (
        P(("dp", "tensor"), None),
        P(("dp", "tensor"), None),
        P("dp", None),
        P(),
        P("dp", "tensor"),
        P("dp", "tensor"),
        P("dp", "tensor"),
        P(),
        P("tensor", "dp"),
        P(),
        P("dp", "tensor"),
        P(),
        P("tensor", "dp"),
        P(),
    )
    return jax.shard_map(
        body,
        mesh=mesh,
        in_specs=placed,
        out_specs=(
            P(("dp", "tensor"), None),
            P(("dp", "tensor"), None),
            P(),
            P("dp", "tensor"),
            P("dp", "tensor"),
            P("dp", "tensor"),
            P(),
            P("tensor", "dp"),
            P(),
            P("dp", "tensor"),
            P(),
            P("tensor", "dp"),
            P(),
        ),
        check_vma=False,
    )
```

profile of v0, /device:TPU:0, one launch (start us, length us, event | category | flops | bytes accessed | tf_op | source)
XLA Modules:
  0.0 1192.5 jit_solution(7304467710094383496)
XLA Ops:
  13.7 34.5 %all_gather.35 = bf16[1280,320]{1,0:T(8,128)(2,1)S(1)} all-gather(bf16[160,320]{1,0:T(8,128)(2,1)S(1)} %copy-done.32), channel_id=1, replica_groups=mesh['dp'=8,'tensor'=4] {'dp'}, dimensions={0}, use_global_device_ids=true | all-gather | bytes 921600 | tf_op jit(solution)/shard_map/all_gather | solution.py:116
  48.2 34.5 %all_gather.36 = bf16[1280,320]{1,0:T(8,128)(2,1)} all-gather(bf16[160,320]{1,0:T(8,128)(2,1)S(1)} %copy-done.33), channel_id=1, replica_groups=mesh['dp'=8,'tensor'=4] {'dp'}, dimensions={0}, use_global_device_ids=true | all-gather | bytes 921600 | tf_op jit(solution)/shard_map/all_gather | solution.py:117
  82.7 35.3 %all_gather.37 = bf16[1280,320]{1,0:T(8,128)(2,1)} all-gather(bf16[160,320]{1,0:T(8,128)(2,1)S(1)} %copy-done.34), channel_id=1, replica_groups=mesh['dp'=8,'tensor'=4] {'dp'}, dimensions={0}, use_global_device_ids=true | all-gather | bytes 921600 | tf_op jit(solution)/shard_map/all_gather | solution.py:118
  118.0 34.0 %all_gather.38 = bf16[320,1280]{0,1:T(8,128)(2,1)} all-gather(bf16[320,160]{0,1:T(8,128)(2,1)S(1)} %copy-done.35), channel_id=1, replica_groups=mesh['dp'=8,'tensor'=4] {'dp'}, dimensions={1}, use_global_device_ids=true | all-gather | bytes 921600 | tf_op jit(solution)/shard_map/all_gather | solution.py:119
  171.4 57.9 %while.27 = (s32[]{:T(128)}, bf16[4,512,4,80]{1,3,2,0:T(8,128)(2,1)}, f32[4,4,512,1]{2,1,3,0:T(4,128)S(1)}, s32[4,512]{1,0:T(4,128)S(1)}, s32[1,2048]{1,0:T(1,12...) while((s32[]{:T(128)}, ...), condition=%wide.region_4.5_spmd, body=%wide.region_1.4_spmd.sunk | while | flops 1381136384 | bytes 57882740 | solution.py:47
  239.7 34.6 %all_gather.39 = bf16[1280,320]{1,0:T(8,128)(2,1)} all-gather(bf16[160,320]{1,0:T(8,128)(2,1)S(1)} %copy-done.36), channel_id=1, replica_groups=mesh['dp'=8,'tensor'=4] {'dp'}, dimensions={0}, use_global_device_ids=true | all-gather | bytes 921600 | tf_op jit(solution)/shard_map/all_gather | solution.py:120
  276.6 34.0 %all_gather.41 = bf16[320,1280]{0,1:T(8,128)(2,1)} all-gather(bf16[320,160]{0,1:T(8,128)(2,1)S(1)} %copy-done.37), channel_id=1, replica_groups=mesh['dp'=8,'tensor'=4] {'dp'}, dimensions={1}, use_global_device_ids=true | all-gather | bytes 921600 | tf_op jit(solution)/shard_map/all_gather | solution.py:121
  312.9 12.8 %reduce-scatter.15.cloned.1.call-done = f32[512,1280]{1,0:T(8,128)} async-done(((f32[2048,1280]{1,0:T(8,128)}), f32[512,1280]{1,0:T(8,128)}) %reduce-scatter.15.cloned.1.call-update) | async-done | bytes 2621456 | tf_op jit(solution)/shard_map/reduce_scatter | solution.py:152
  329.7 26.9 %all-gather.7.cloned.1.call-done = bf16[1280,1280]{0,1:T(8,128)(2,1)} async-done(((bf16[1280,320]{0,1:T(8,128)(2,1)}), bf16[1280,1280]{0,1:T(8,128)(2,1)}) %all-gather.7.cloned.1.call-update) | async-done | bytes 3276816 | tf_op jit(solution)/shard_map/all_gather | solution.py:161
  362.8 25.1 %all-gather.9.cloned.1.call-done = bf16[1280,1280]{1,0:T(8,128)(2,1)} async-done(((bf16[320,1280]{1,0:T(8,128)(2,1)}), bf16[1280,1280]{1,0:T(8,128)(2,1)}) %all-gather.9.cloned.1.call-update) | async-done | bytes 3276816 | tf_op jit(solution)/shard_map/all_gather | solution.py:162
  415.9 24.7 %all-gather.11.cloned.1.call-done = bf16[2048,1280]{1,0:T(8,128)(2,1)} async-done(((bf16[512,1280]{1,0:T(8,128)(2,1)}), bf16[2048,1280]{1,0:T(8,128)(2,1)}) %all-gather.11.cloned.1.call-update) | async-done | bytes 5242896 | tf_op jit(solution)/shard_map/all_gather | solution.py:195
  453.4 203.8 %while.28 = (s32[]{:T(128)}, f32[2048,4,80]{0,2,1:T(8,128)}, f32[2048,4,80]{0,2,1:T(8,128)}, f32[4,512,4,80]{1,3,2,0:T(8,128)}, bf16[4,512,4,80]{1,3,2,0:T(8,128...) while((s32[]{:T(128)}, f32[2048,4,80]{0,2,1:T(8,128)}, ...), condition=%wide.region_10.11_spmd.clone, body=%wide.region_8.10_spmd.clone.sunk | while | flops 3409442816 | bytes 245045552 | solution.py:86
  472.2 12.5 %multiply_reduce_fusion.6 = (f32[4,512]{1,0:T(4,128)S(1)}, f32[4,512,2048]{2,1,0:T(8,128)}) fusion(f32[4,512,2048]{2,1,0:T(8,128)} %copy-done, f32[4,512]{1,0:T(4,128)S(1)} %dynamic-slice_bitcast_fusion.2, pred[512,2048]{1,0:T(8,128)(4,1)S(1)} %broadcast_compare_fusion.5, bf16[2048,4,80]{0,2,1:T(8,128)(2,1)} %copy-done.6, ...), kind=kOutput, calls=%fused_computation.17.clone.1 | convolution fusion | flops 687863808 | bytes 36257796 | tf_op jit(solution)/shard_map/while/body/eval_jaxpr/qhd,khd->hqk/dot_general | solution.py:72
  484.7 12.4 %multiply_convert_fusion.12 = bf16[4,512,2048]{2,1,0:T(8,128)(2,1)S(1)} fusion(f32[4,512,2048]{2,1,0:T(8,128)} %get-tuple-element.432, f32[4,512,2048]{2,1,0:T(8,128)} %copy-done, f32[4,512]{1,0:T(4,128)S(1)} %get-tuple-element.433, f32[4,512]{1,0:T(4,128)S(1)} %dynamic-slice_bitcast_fusion.2, pred[512,2048]{1,0:T(8,128)(4,1)S(1)} %broadcast_compare_fusion.5), kind=kLoop, calls=%fused_computation.16.clone.1 | loop fusion | flops 20971520 | bytes 43008000 | tf_op jit(solution)/shard_map/while/body/eval_jaxpr/convert_element_type | solution.py:76
  508.6 8.3 copy-done
  516.9 8.1 fusion.135
  525.0 13.5 %multiply_reduce_fusion.6 = (f32[4,512]{1,0:T(4,128)S(1)}, f32[4,512,2048]{2,1,0:T(8,128)}) fusion(f32[4,512,2048]{2,1,0:T(8,128)} %copy-done, f32[4,512]{1,0:T(4,128)S(1)} %dynamic-slice_bitcast_fusion.2, pred[512,2048]{1,0:T(8,128)(4,1)S(1)} %broadcast_compare_fusion.5, bf16[2048,4,80]{0,2,1:T(8,128)(2,1)} %copy-done.6, ...), kind=kOutput, calls=%fused_computation.17.clone.1 | convolution fusion | flops 687863808 | bytes 36257796 | tf_op jit(solution)/shard_map/while/body/eval_jaxpr/qhd,khd->hqk/dot_general | solution.py:72
  538.6 12.4 %multiply_convert_fusion.12 = bf16[4,512,2048]{2,1,0:T(8,128)(2,1)S(1)} fusion(f32[4,512,2048]{2,1,0:T(8,128)} %get-tuple-element.432, f32[4,512,2048]{2,1,0:T(8,128)} %copy-done, f32[4,512]{1,0:T(4,128)S(1)} %get-tuple-element.433, f32[4,512]{1,0:T(4,128)S(1)} %dynamic-slice_bitcast_fusion.2, pred[512,2048]{1,0:T(8,128)(4,1)S(1)} %broadcast_compare_fusion.5), kind=kLoop, calls=%fused_computation.16.clone.1 | loop fusion | flops 20971520 | bytes 43008000 | tf_op jit(solution)/shard_map/while/body/eval_jaxpr/convert_element_type | solution.py:76
  568.3 7.9 fusion.135
  576.2 12.5 %multiply_reduce_fusion.6 = (f32[4,512]{1,0:T(4,128)S(1)}, f32[4,512,2048]{2,1,0:T(8,128)}) fusion(f32[4,512,2048]{2,1,0:T(8,128)} %copy-done, f32[4,512]{1,0:T(4,128)S(1)} %dynamic-slice_bitcast_fusion.2, pred[512,2048]{1,0:T(8,128)(4,1)S(1)} %broadcast_compare_fusion.5, bf16[2048,4,80]{0,2,1:T(8,128)(2,1)} %copy-done.6, ...), kind=kOutput, calls=%fused_computation.17.clone.1 | convolution fusion | flops 687863808 | bytes 36257796 | tf_op jit(solution)/shard_map/while/body/eval_jaxpr/qhd,khd->hqk/dot_general | solution.py:72
  588.7 12.1 %multiply_convert_fusion.12 = bf16[4,512,2048]{2,1,0:T(8,128)(2,1)S(1)} fusion(f32[4,512,2048]{2,1,0:T(8,128)} %get-tuple-element.432, f32[4,512,2048]{2,1,0:T(8,128)} %copy-done, f32[4,512]{1,0:T(4,128)S(1)} %get-tuple-element.433, f32[4,512]{1,0:T(4,128)S(1)} %dynamic-slice_bitcast_fusion.2, pred[512,2048]{1,0:T(8,128)(4,1)S(1)} %broadcast_compare_fusion.5), kind=kLoop, calls=%fused_computation.16.clone.1 | loop fusion | flops 20971520 | bytes 43008000 | tf_op jit(solution)/shard_map/while/body/eval_jaxpr/convert_element_type | solution.py:76
  626.0 12.5 %multiply_reduce_fusion.6 = (f32[4,512]{1,0:T(4,128)S(1)}, f32[4,512,2048]{2,1,0:T(8,128)}) fusion(f32[4,512,2048]{2,1,0:T(8,128)} %copy-done, f32[4,512]{1,0:T(4,128)S(1)} %dynamic-slice_bitcast_fusion.2, pred[512,2048]{1,0:T(8,128)(4,1)S(1)} %broadcast_compare_fusion.5, bf16[2048,4,80]{0,2,1:T(8,128)(2,1)} %copy-done.6, ...), kind=kOutput, calls=%fused_computation.17.clone.1 | convolution fusion | flops 687863808 | bytes 36257796 | tf_op jit(solution)/shard_map/while/body/eval_jaxpr/qhd,khd->hqk/dot_general | solution.py:72
  638.5 12.1 %multiply_convert_fusion.12 = bf16[4,512,2048]{2,1,0:T(8,128)(2,1)S(1)} fusion(f32[4,512,2048]{2,1,0:T(8,128)} %get-tuple-element.432, f32[4,512,2048]{2,1,0:T(8,128)} %copy-done, f32[4,512]{1,0:T(4,128)S(1)} %get-tuple-element.433, f32[4,512]{1,0:T(4,128)S(1)} %dynamic-slice_bitcast_fusion.2, pred[512,2048]{1,0:T(8,128)(4,1)S(1)} %broadcast_compare_fusion.5), kind=kLoop, calls=%fused_computation.16.clone.1 | loop fusion | flops 20971520 | bytes 43008000 | tf_op jit(solution)/shard_map/while/body/eval_jaxpr/convert_element_type | solution.py:76
  671.1 9.3 add_add_fusion
  725.3 39.7 %reduce-scatter.17.cloned.1.call-done = f32[512,1280]{1,0:T(8,128)} async-done(((f32[2048,1280]{1,0:T(8,128)}), f32[512,1280]{1,0:T(8,128)}) %reduce-scatter.17.cloned.1.call-update) | async-done | bytes 2621456 | tf_op jit(solution)/shard_map/reduce_scatter | solution.py:229
  772.8 41.1 %all-reduce = (f32[1280]{0:T(1024)}, f32[80]{0:T(128)}, f32[1280]{0:T(1024)}, f32[1280]{0:T(1024)}, f32[1280]{0:T(1024)}) all-reduce(f32[1280]{0:T(1024)S(1)} %get-tuple-element.254, f32[80]{0:T(128)S(1)} %divide_multiply_fusion, f32[1280]{0:T(1024)S(1)} %copy-done.47, ...), channel_id=1, replica_groups=mesh['dp'=8,'tensor'=4] {'dp','tensor'}, use_global_device_ids=true, to_apply=%region_14.15 | all-reduce | flops 5200 | bytes 41600 | tf_op jit(solution)/shard_map/psum | solution.py:246
  813.9 22.1 %reduce-scatter.25.cloned.1.call-done = f32[320,160]{0,1:T(8,128)} async-done(((f32[320,1280]{0,1:T(8,128)}), f32[320,160]{0,1:T(8,128)}) %reduce-scatter.25.cloned.1.call-update) | async-done | bytes 204816 | tf_op jit(solution)/shard_map/reduce_scatter | solution.py:242
  836.0 69.9 %reduce-scatter.23.cloned.1.call-done = f32[160,320]{1,0:T(8,128)} async-done(((f32[1280,320]{1,0:T(8,128)}), f32[160,320]{1,0:T(8,128)}) %reduce-scatter.23.cloned.1.call-update) | async-done | bytes 204816 | tf_op jit(solution)/shard_map/reduce_scatter | solution.py:241
  905.9 69.9 %reduce-scatter.21.cloned.1.call-done = f32[160,320]{1,0:T(8,128)} async-done(((f32[1280,320]{1,0:T(8,128)}), f32[160,320]{1,0:T(8,128)}) %reduce-scatter.21.cloned.1.call-update) | async-done | bytes 204816 | tf_op jit(solution)/shard_map/reduce_scatter | solution.py:240
  975.8 70.1 %reduce-scatter.19.cloned.1.call-done = f32[160,320]{1,0:T(8,128)} async-done(((f32[1280,320]{1,0:T(8,128)}), f32[160,320]{1,0:T(8,128)}) %reduce-scatter.19.cloned.1.call-update) | async-done | bytes 204816 | tf_op jit(solution)/shard_map/reduce_scatter | solution.py:239
  1045.9 69.8 %reduce-scatter.33.cloned.1.call-done = f32[160,320]{1,0:T(8,128)} async-done(((f32[1280,320]{1,0:T(8,128)}), f32[160,320]{1,0:T(8,128)}) %reduce-scatter.33.cloned.1.call-update) | async-done | bytes 204816
  1115.7 70.1 %reduce-scatter.31.cloned.1.call-done = f32[160,320]{1,0:T(8,128)} async-done(((f32[1280,320]{1,0:T(8,128)}), f32[160,320]{1,0:T(8,128)}) %reduce-scatter.31.cloned.1.call-update) | async-done | bytes 204816
  (279 shorter events, 293.8 us)
Async XLA Ops:
  7.2 144.7 %all-gather.5.cloned.1.call-start = ((), (), s32[]{:S(2)}) async-start(), calls=%async_computation.10 | async-start | bytes 6553600 | tf_op jit(solution)/shard_map/all_gather | solution.py:131
  8.9 39.2 %copy-start.33 = (bf16[160,320]{1,0:T(8,128)(2,1)S(1)}, bf16[160,320]{1,0:T(8,128)(2,1)}, u32[]{:S(2)}) copy-start(bf16[160,320]{1,0:T(8,128)(2,1)} %param.23) | copy-start | bytes 307204
  9.5 73.1 %copy-start.34 = (bf16[160,320]{1,0:T(8,128)(2,1)S(1)}, bf16[160,320]{1,0:T(8,128)(2,1)}, u32[]{:S(2)}) copy-start(bf16[160,320]{1,0:T(8,128)(2,1)} %param.24) | copy-start | bytes 307204
  12.3 105.7 %copy-start.35 = (bf16[320,160]{0,1:T(8,128)(2,1)S(1)}, bf16[320,160]{0,1:T(8,128)(2,1)}, u32[]{:S(2)}) copy-start(bf16[320,160]{0,1:T(8,128)(2,1)} %param.26) | copy-start | bytes 307204
  12.3 313.4 %reduce-scatter.15.cloned.1.call-start = ((), (), s32[]{:S(2)}) async-start(), calls=%async_computation.11 | async-start | bytes 13107200 | tf_op jit(solution)/shard_map/reduce_scatter | solution.py:152
  13.6 147.7 %copy-start.48 = (f32[80]{0:T(128)}, f32[80]{0:T(128)S(1)}, u32[]{:S(2)}) copy-start(f32[80]{0:T(128)S(1)} %log-plus-one_multiply_fusion) | copy-start | bytes 964
  48.2 103.8 %copy-start.26 = (bf16[1280,320]{1,0:T(8,128)(2,1)}, bf16[1280,320]{1,0:T(8,128)(2,1)S(1)}, u32[]{:S(2)}) copy-start(bf16[1280,320]{1,0:T(8,128)(2,1)S(1)} %all_gather.35) | copy-start | bytes 2457604
  238.8 37.8 %copy-start.37 = (bf16[320,160]{0,1:T(8,128)(2,1)S(1)}, bf16[320,160]{0,1:T(8,128)(2,1)}, u32[]{:S(2)}) copy-start(bf16[320,160]{0,1:T(8,128)(2,1)} %param.30) | copy-start | bytes 307204
  238.8 117.8 %all-gather.7.cloned.1.call-start = ((), (), s32[]{:S(2)}) async-start(), calls=%async_computation.12 | async-start | bytes 4096000 | tf_op jit(solution)/shard_map/all_gather | solution.py:161
  276.6 111.4 %all-gather.9.cloned.1.call-start = ((), (), s32[]{:S(2)}) async-start(), calls=%async_computation.13 | async-start | bytes 4096000 | tf_op jit(solution)/shard_map/all_gather | solution.py:162
  312.8 43.8 %copy-start.30 = (f32[1280]{0:T(1024)S(1)}, f32[1280]{0:T(1024)}, u32[]{:S(2)}) copy-start(f32[1280]{0:T(1024)} %param.27) | copy-start | bytes 15364
  312.8 43.8 %copy-start.51 = (f32[1280]{0:T(1024)S(1)}, f32[1280]{0:T(1024)}, u32[]{:S(2)}) copy-start(f32[1280]{0:T(1024)} %param.29) | copy-start | bytes 15364
  312.8 127.7 %all-gather.11.cloned.1.call-start = ((), (), s32[]{:S(2)}) async-start(), calls=%async_computation.14 | async-start | bytes 6553600 | tf_op jit(solution)/shard_map/all_gather | solution.py:195
  329.7 78.4 %copy-start.39 = (f32[512]{0:T(512)}, f32[512]{0:T(512)S(1)}, u32[]{:S(2)}) copy-start(f32[512]{0:T(512)S(1)} %add_rsqrt_fusion) | copy-start | bytes 6148
  400.0 312.0 %reduce-scatter.29.cloned.1.call-start = ((), (), s32[]{:S(2)}) async-start(), calls=%async_computation.21 | async-start | bytes 8192000 | tf_op jit(solution)/shard_map/reduce_scatter | solution.py:191
  406.8 308.1 %reduce-scatter.27.cloned.1.call-start = ((), (), s32[]{:S(2)}) async-start(), calls=%async_computation.20 | async-start | bytes 8192000 | tf_op jit(solution)/shard_map/reduce_scatter | solution.py:190
  415.8 349.1 %reduce-scatter.17.cloned.1.call-start = ((), (), s32[]{:S(2)}) async-start(), calls=%async_computation.15 | async-start | bytes 13107200 | tf_op jit(solution)/shard_map/reduce_scatter | solution.py:229
  484.7 12.4 %copy-start.1 = (f32[2048,4,80]{0,2,1:T(8,128)S(1)}, f32[2048,4,80]{0,2,1:T(8,128)}, u32[]{:S(2)}) copy-start(f32[2048,4,80]{0,2,1:T(8,128)} %get-tuple-element.475) | copy-start | bytes 7864324 | tf_op jit(solution)/shard_map/while
  538.6 12.4 %copy-start.1 = (f32[2048,4,80]{0,2,1:T(8,128)S(1)}, f32[2048,4,80]{0,2,1:T(8,128)}, u32[]{:S(2)}) copy-start(f32[2048,4,80]{0,2,1:T(8,128)} %get-tuple-element.475) | copy-start | bytes 7864324 | tf_op jit(solution)/shard_map/while
  588.7 12.1 %copy-start.1 = (f32[2048,4,80]{0,2,1:T(8,128)S(1)}, f32[2048,4,80]{0,2,1:T(8,128)}, u32[]{:S(2)}) copy-start(f32[2048,4,80]{0,2,1:T(8,128)} %get-tuple-element.475) | copy-start | bytes 7864324 | tf_op jit(solution)/shard_map/while
  638.5 12.1 %copy-start.1 = (f32[2048,4,80]{0,2,1:T(8,128)S(1)}, f32[2048,4,80]{0,2,1:T(8,128)}, u32[]{:S(2)}) copy-start(f32[2048,4,80]{0,2,1:T(8,128)} %get-tuple-element.475) | copy-start | bytes 7864324 | tf_op jit(solution)/shard_map/while
  680.4 155.5 %reduce-scatter.25.cloned.1.call-start = ((), (), s32[]{:S(2)}) async-start(), calls=%async_computation.19 | async-start | bytes 2211840 | tf_op jit(solution)/shard_map/reduce_scatter | solution.py:242
  688.5 217.4 %reduce-scatter.23.cloned.1.call-start = ((), (), s32[]{:S(2)}) async-start(), calls=%async_computation.18 | async-start | bytes 2211840 | tf_op jit(solution)/shard_map/reduce_scatter | solution.py:241
  696.5 279.3 %reduce-scatter.21.cloned.1.call-start = ((), (), s32[]{:S(2)}) async-start(), calls=%async_computation.17 | async-start | bytes 2211840 | tf_op jit(solution)/shard_map/reduce_scatter | solution.py:240
  704.0 341.9 %reduce-scatter.19.cloned.1.call-start = ((), (), s32[]{:S(2)}) async-start(), calls=%async_computation.16 | async-start | bytes 2211840 | tf_op jit(solution)/shard_map/reduce_scatter | solution.py:239
  711.9 403.8 %reduce-scatter.33.cloned.1.call-start = ((), (), s32[]{:S(2)}) async-start(), calls=%async_computation.23 | async-start | bytes 2211840
  714.8 470.9 %reduce-scatter.31.cloned.1.call-start = ((), (), s32[]{:S(2)}) async-start(), calls=%async_computation.22 | async-start | bytes 2211840
  724.2 40.8 %copy-start.38 = (f32[1280]{0:T(1024)S(1)}, f32[1280]{0:T(1024)}, u32[]{:S(2)}) copy-start(f32[1280]{0:T(1024)} %param.21) | copy-start | bytes 15364
  724.2 40.8 %copy-start.42 = (f32[512]{0:T(512)S(1)}, f32[512]{0:T(512)}, u32[]{:S(2)}) copy-start(f32[512]{0:T(512)} %copy-done.41) | copy-start | bytes 6148
  725.2 42.8 %copy-start.31 = (f32[1280]{0:T(1024)S(1)}, f32[1280]{0:T(1024)}, u32[]{:S(2)}) copy-start(f32[1280]{0:T(1024)} %param.27) | copy-start | bytes 15364
  725.2 42.7 %copy-start.40 = (f32[512]{0:T(512)S(1)}, f32[512]{0:T(512)}, u32[]{:S(2)}) copy-start(f32[512]{0:T(512)} %copy-done.39) | copy-start | bytes 6148
  725.2 42.7 %copy-start.44 = (f32[512]{0:T(512)S(1)}, f32[512]{0:T(512)}, u32[]{:S(2)}) copy-start(f32[512]{0:T(512)} %copy-done.43) | copy-start | bytes 6148
  (54 other events, 200.9 us)
Sparse Core Ops, SparseCore 0:
  12.5 43.1 all-gather.4
  238.9 86.7 reduce-scatter.14
  327.3 29.2 all-gather.6
  358.6 29.2 all-gather.8
  400.1 40.4 all-gather.10
  443.0 60.1 reduce-scatter.28
  505.8 60.1 reduce-scatter.26
  680.5 84.3 reduce-scatter.16
  769.0 66.9 reduce-scatter.24
  840.3 65.5 reduce-scatter.22
  910.0 65.7 reduce-scatter.20
  980.1 65.7 reduce-scatter.18
  1050.0 65.6 reduce-scatter.32
  1120.0 65.7 reduce-scatter.30
where the time goes:
time: 1200 us; the launch traced here: 1190 us
  waiting for transfers between devices  501 us (42%)
  matrix products  264 us (22%)
  blocking collectives  248 us (21%)
  other arithmetic  94.6 us (8%)
  local copies, waits for them, and re-layouts  67.5 us (6%)
  between operations  14.7 us (1%)
    unnamed x16, waiting for transfers between devices  140 us
    reduce_scatter x1, waiting for transfers between devices, body(): lax.psum_scatter(grad_query, 'dp', scatter_dimension=0, tiled=True)  70.1 us
    reduce_scatter x1, waiting for transfers between devices, body(): lax.psum_scatter(grad_value, 'dp', scatter_dimension=0, tiled=True)  69.9 us
    reduce_scatter x1, waiting for transfers between devices, body(): lax.psum_scatter(grad_key, 'dp', scatter_dimension=0, tiled=True)  69.9 us
    dot_general x4, matrix products, one_block(): jnp.einsum('qhd,khd->hqk', grad_block, value_all, preferred_element_type=...  50.9 us
    convert_element_type x4, other arithmetic, one_block(): grad_scores = (probs * (grad_probs - inner)).astype(jnp.bfloat16)  49 us
    psum x1, blocking collectives, body(): lax.psum((grad_attn_gain, grad_scale, grad_mlp_gain, bias_full, jnp.sum(c...  41.1 us
    reduce_scatter x1, waiting for transfers between devices, body(): lax.psum_scatter(total_grad + jnp.einsum('gc,dc->gd', grad_value_rows, ba...  39.7 us
  transfers between devices with their start and end apart: 14, of which 11 were waited for; matrix products, arithmetic and copies ran while one was open for 24% of the time, Pallas kernels for 0%

commit v1 on v0

v1 whole, which is shorter than its diff:
```python
import math

import jax
import jax.numpy as jnp
from jax import lax
from jax.experimental import pallas as pl
from jax.experimental.pallas import tpu as pltpu
from jax.sharding import PartitionSpec as P

HD = 80
HP = 128
TILE = 256
BLOCK_MOST = 256
EPSILON = 1e-06
SCORE_BASE = 1.442695041
MASKED = -1e30
BF = jnp.bfloat16
F32 = jnp.float32


def mm(a, b, ca, cb):
    return lax.dot_general(a, b, (((ca,), (cb,)), ((), ())), preferred_element_type=F32)


def reach(tile, length):
    return min((tile + 1) * TILE + BLOCK_MOST, length)


def attend_kernel(q_ref, k_ref, v_ref, idr_ref, idc_ref, o_ref, lse_ref, vt_ref):
    length = q_ref.shape[0]
    tiles = length // TILE
    sub = lax.broadcasted_iota(jnp.int32, (HP, length), 0)
    vt_ref[...] = jnp.where(sub == HD, 1.0, v_ref[...].astype(F32).T).astype(BF)

    def scores(t):
        seen, low = reach(t, length), t * TILE
        st = mm(k_ref[:seen, :], q_ref[low : low + TILE, :], 1, 1)
        visible = idc_ref[low:seen, :] <= idr_ref[:, low : low + TILE]
        masked = jnp.where(visible, st[low:], MASKED)
        return jnp.concatenate([st[:low], masked], 0) if low else masked

    st = scores(0)
    for t in range(tiles):
        later = scores(t + 1) if t + 1 < tiles else None
        seen, low = st.shape[0], t * TILE
        group = jnp.max(st.reshape(seen // 64, 64, TILE), axis=0)
        highest = jnp.max(group, axis=0, keepdims=True)
        weights = jnp.exp(st - highest).astype(BF)
        ot = mm(vt_ref[:, :seen], weights, 1, 0)
        summed = ot[HD : HD + 1, :]
        o_ref[low : low + TILE, :] = (ot * (1.0 / summed)).T.astype(BF)
        lse_ref[0, :, low : low + TILE] = highest + jnp.log(summed)
        st = later


def attend(q, k, v, idr, idc):
    length, wide = q.shape
    heads = wide // HP
    col = pl.BlockSpec((length, HP), lambda h: (0, h))
    return pl.pallas_call(
        attend_kernel,
        grid=(heads,),
        out_shape=[
            jax.ShapeDtypeStruct((length, wide), BF),
            jax.ShapeDtypeStruct((heads, 1, length), F32),
        ],
        in_specs=[
            col,
            col,
            col,
            pl.BlockSpec((1, length), lambda h: (0, 0)),
            pl.BlockSpec((length, 1), lambda h: (0, 0)),
        ],
        out_specs=[col, pl.BlockSpec((1, 1, length), lambda h: (h, 0, 0))],
        scratch_shapes=[pltpu.VMEM((HP, length), BF)],
        compiler_params=pltpu.CompilerParams(vmem_limit_bytes=56 << 20),
        cost_estimate=pl.CostEstimate(
            flops=heads * length * length * 2 * 256 * 2, bytes_accessed=8 << 20, transcendentals=0
        ),
    )(q, k, v, idr, idc)


def attend_back_kernel(
    q_ref, k_ref, v_ref, o_ref, do_ref, lse_ref, fac_ref, idr_ref, idc_ref,
    dq_ref, dk_ref, dv_ref, qs_ref, dka, dva, kt_ref,
):
    length = q_ref.shape[0]
    tiles = length // TILE
    kt_ref[...] = k_ref[...].astype(F32).T.astype(BF)
    dka[...] = jnp.zeros_like(dka)
    dva[...] = jnp.zeros_like(dva)
    scale_sum = jnp.zeros((1, HP), F32)
    for t in range(tiles):
        seen, low = reach(t, length), t * TILE
        rows = slice(low, low + TILE)
        qt = q_ref[rows, :]
        dot_ = do_ref[rows, :]
        delta = jnp.sum((dot_.astype(F32) * o_ref[rows, :].astype(F32)).T, axis=0, keepdims=True)
        st = mm(k_ref[:seen, :], qt, 1, 1)
        p = jnp.exp(st - lse_ref[0, :, rows])
        visible = idc_ref[low:seen, :] <= idr_ref[:, rows]
        pm = jnp.where(visible, p[low:], 0.0)
        p = jnp.concatenate([p[:low], pm], 0) if low else pm
        dp = mm(v_ref[:seen, :], dot_, 1, 1)
        ds = (p * (dp - delta)).astype(BF)
        dva[:seen, :] += mm(p.astype(BF), dot_, 1, 0)
        dka[:seen, :] += mm(ds, qt, 1, 0)
        dq = mm(kt_ref[:, :seen], ds, 1, 0).T
        scale_sum = scale_sum + jnp.sum(dq * qt.astype(F32), axis=0, keepdims=True)
        dq_ref[rows, :] = (dq * fac_ref[...]).astype(BF)
    dk_ref[...] = dka[...].astype(BF)
    dv_ref[...] = dva[...].astype(BF)
    qs_ref[0] = scale_sum


def attend_back(q, k, v, o, do, lse, factor, idr, idc):
    length, wide = q.shape
    heads = wide // HP
    col = pl.BlockSpec((length, HP), lambda h: (0, h))
    return pl.pallas_call(
        attend_back_kernel,
        grid=(heads,),
        out_shape=[jax.ShapeDtypeStruct((length, wide), BF)] * 3
        + [jax.ShapeDtypeStruct((heads, 1, HP), F32)],
        in_specs=[
            col, col, col, col, col,
            pl.BlockSpec((1, 1, length), lambda h: (h, 0, 0)),
            pl.BlockSpec((1, HP), lambda h: (0, 0)),
            pl.BlockSpec((1, length), lambda h: (0, 0)),
            pl.BlockSpec((length, 1), lambda h: (0, 0)),
        ],
        out_specs=[col, col, col, pl.BlockSpec((1, 1, HP), lambda h: (h, 0, 0))],
        scratch_shapes=[pltpu.VMEM((length, HP), F32)] * 2 + [pltpu.VMEM((HP, length), BF)],
        compiler_params=pltpu.CompilerParams(vmem_limit_bytes=56 << 20),
        cost_estimate=pl.CostEstimate(
            flops=heads * length * length * 2 * 256 * 4, bytes_accessed=16 << 20, transcendentals=0
        ),
    )(q, k, v, o, do, lse, factor, idr, idc)


def swap(v, axis, size, mask):
    return lax.ppermute(v, axis, [(i, i ^ mask) for i in range(size)])


def gather_dp(shard, size):
    if size != 8:
        return lax.all_gather(shard, "dp", axis=0)
    far, here = size // 2, lax.axis_index("dp")
    major, minor = here // 2, here % 2
    parts = [shard]
    for step in range(1, far):
        parts.append(
            lax.ppermute(shard, "dp", [(i, (i + 2 * step) % size) for i in range(size)])
        )
    others = [swap(part, "dp", size, 1) for part in parts]
    whole = jnp.zeros((size,) + shard.shape, shard.dtype)
    for step in range(far):
        source = ((major + far - step) % far) * 2
        whole = lax.dynamic_update_slice(whole, parts[step][None], (source + minor, 0, 0))
        whole = lax.dynamic_update_slice(whole, others[step][None], (source + 1 - minor, 0, 0))
    return whole


def scatter_dp(grad, size):
    if size != 8:
        return lax.psum_scatter(grad, "dp", scatter_dimension=0, tiled=False)
    far, here = size // 2, lax.axis_index("dp")
    major, minor = here // 2, here % 2
    split = grad.reshape((far, 2) + grad.shape[1:])
    mine = lax.dynamic_index_in_dim(split, minor, 1, keepdims=False)
    theirs = lax.dynamic_index_in_dim(split, 1 - minor, 1, keepdims=False)
    half = mine + swap(theirs.astype(BF), "dp", size, 1).astype(F32)
    total = lax.dynamic_index_in_dim(half, major, 0, keepdims=False)
    for step in range(1, far):
        piece = lax.dynamic_index_in_dim(half, (major + step) % far, 0, keepdims=False)
        total = total + lax.ppermute(
            piece.astype(BF), "dp", [(i, (i + 2 * step) % size) for i in range(size)]
        ).astype(F32)
    return total


def sum_all(v, dp, tensor):
    if dp != 8:
        return lax.psum(v, ("dp", "tensor"))
    v = v + swap(v, "tensor", tensor, 1)
    v = v + swap(v, "tensor", tensor, 2)
    v = v + swap(v, "dp", dp, 1)
    parts = [lax.ppermute(v, "dp", [(i, (i + 2 * s) % dp) for i in range(dp)]) for s in (1, 2, 3)]
    here = lax.axis_index("dp") // 2
    stack = jnp.zeros((4,) + v.shape, v.dtype)
    for s, part in enumerate([v] + parts):
        stack = lax.dynamic_update_slice(stack, part[None], ((here + 4 - s) % 4,) + (0,) * v.ndim)
    return (stack[0] + stack[1]) + (stack[2] + stack[3])


def pad_heads(w):
    rows, cols = w.shape
    w = w.reshape(rows, cols // HD, HD)
    return jnp.pad(w, ((0, 0), (0, 0), (0, HP - HD))).reshape(rows, cols // HD * HP)


def trim_heads(w):
    rows, cols = w.shape
    return w.reshape(rows, cols // HP, HP)[:, :, :HD].reshape(rows, cols // HP * HD)


def rms_stats(v):
    inverse = lax.rsqrt(jnp.mean(v * v, axis=-1, keepdims=True) + EPSILON)
    return v * inverse, inverse


def rms_back(grad, hat, inverse, gain):
    scaled = grad * gain
    return inverse * (scaled - hat * jnp.mean(scaled * hat, axis=-1, keepdims=True))


def body(dp, tensor, tokens, cotangent, block_ids, attn_gain, w_query, w_key, w_value,
         query_scale, w_out, mlp_gain, w_up, b_up, w_down, b_down):
    assert tensor == 4
    here = lax.axis_index("tensor")
    rows, width = tokens.shape
    length = rows * tensor
    cols = w_query.shape[1]
    heads = cols // HD
    order = [here, here ^ 2, here ^ 1, here ^ 3]

    tokens_f32 = tokens.astype(F32)
    hat_one, inverse_one = rms_stats(tokens_f32)
    normed_own = (hat_one * attn_gain).astype(BF)
    normed_x = swap(normed_own, "tensor", tensor, 2)
    blocks = [normed_own, normed_x, swap(normed_own, "tensor", tensor, 1)]
    blocks.append(swap(normed_x, "tensor", tensor, 1))
    normed = jnp.zeros((length, width), BF)
    for at, block in zip(order, blocks):
        normed = lax.dynamic_update_slice(normed, block, (at * rows, 0))

    first = jnp.concatenate([w_query, w_key, w_value], axis=1)
    second = jnp.concatenate([w_out.T, w_up, w_down.T], axis=1)
    full_qkv = gather_dp(first, dp).reshape(width, 3 * cols)
    pair = jnp.concatenate([second, swap(second, "tensor", tensor, 2)], axis=1)
    half = gather_dp(pair, dp).reshape(width, 6 * cols)
    both = swap(half, "tensor", tensor, 1)

    def wide(at):
        return jnp.concatenate(
            [
                half[:, at * cols : (at + 1) * cols],
                half[:, (3 + at) * cols : (4 + at) * cols],
                both[:, at * cols : (at + 1) * cols],
                both[:, (3 + at) * cols : (4 + at) * cols],
            ],
            axis=1,
        )

    out_t, up, down_t = wide(0), wide(1), wide(2)
    wq, wk, wv = (pad_heads(full_qkv[:, i * cols : (i + 1) * cols]) for i in range(3))

    softplus = jnp.log1p(jnp.exp(query_scale))
    factor = SCORE_BASE / math.sqrt(HD) * softplus
    factor_pad = jnp.pad(factor, (0, HP - HD))[None, :]
    queries = (mm(normed, wq, 1, 0) * jnp.tile(factor_pad, (1, heads))).astype(BF)
    keys = mm(normed, wk, 1, 0).astype(BF)
    values = mm(normed, wv, 1, 0).astype(BF)
    idr = block_ids
    idc = block_ids.reshape(length, 1)
    attended, lse = attend(queries, keys, values, idr, idc)

    def trade(blocks_of):
        return [
            blocks_of(here),
            swap(blocks_of(order[1]), "tensor", tensor, 2),
            swap(blocks_of(order[2]), "tensor", tensor, 1),
            swap(blocks_of(order[3]), "tensor", tensor, 3),
        ]

    compact = trim_heads(attended)
    mine = jnp.concatenate(
        trade(lambda at: lax.dynamic_slice(compact, (at * rows, 0), (rows, cols))), axis=1
    )
    hidden = tokens_f32 + mm(mine, out_t, 1, 1)

    b_rel = jnp.concatenate([lax.dynamic_slice(b_up, (at * cols,), (cols,)) for at in order])
    cot_f32 = cotangent.astype(F32)
    grad_act = mm(cotangent, down_t, 1, 0)
    hat_two, inverse_two = rms_stats(hidden)
    normed_two = (hat_two * mlp_gain).astype(BF)
    pre = mm(normed_two, up, 1, 0) + b_rel
    sig = jax.nn.sigmoid(pre)
    activation = (pre * sig).astype(BF)
    d_pre = (grad_act * sig * (1.0 + pre * (1.0 - sig))).astype(BF)
    d_normed_two = mm(d_pre, up, 1, 1)
    d_hidden = cot_f32 + rms_back(d_normed_two, hat_two, inverse_two, mlp_gain)
    branch = d_hidden.astype(BF)
    d_mine = mm(branch, out_t, 1, 0).astype(BF)
    received = [
        d_mine[:, :cols],
        swap(d_mine[:, cols : 2 * cols], "tensor", tensor, 2),
        swap(d_mine[:, 2 * cols : 3 * cols], "tensor", tensor, 1),
        swap(d_mine[:, 3 * cols :], "tensor", tensor, 3),
    ]
    d_attended = jnp.zeros((length, cols), BF)
    for at, block in zip(order, received):
        d_attended = lax.dynamic_update_slice(d_attended, block, (at * rows, 0))
    d_attended = pad_heads(d_attended)

    output = (hidden + mm(activation, down_t, 1, 1) + b_down).astype(BF)
    d_down_t = mm(cotangent, activation, 0, 0)
    d_up = mm(normed_two, d_pre, 0, 0)
    d_out_t = mm(branch, mine, 0, 0)
    d_mlp_gain = jnp.sum(d_normed_two * hat_two, axis=0)
    d_b_rel = jnp.sum(d_pre.astype(F32), axis=0)
    d_b_up = jnp.zeros_like(b_up)
    for i, at in enumerate(order):
        d_b_up = lax.dynamic_update_slice(d_b_up, d_b_rel[i * cols : (i + 1) * cols], (at * cols,))
    d_b_down = jnp.sum(cot_f32, axis=0)
    early = sum_all(jnp.stack([d_mlp_gain, d_b_up, d_b_down]), dp, tensor)

    keep = jnp.concatenate([g[:, : 2 * cols] for g in (d_out_t, d_up, d_down_t)], axis=1)
    give = jnp.concatenate([g[:, 2 * cols :] for g in (d_out_t, d_up, d_down_t)], axis=1)
    keep = keep + swap(give.astype(BF), "tensor", tensor, 1).astype(F32)
    kept = scatter_dp(keep.reshape(dp, width // dp, 6 * cols), dp)
    kept = kept.reshape(width // dp, 3, 2, cols)
    second_grads = kept[:, :, 0] + swap(kept[:, :, 1].astype(BF), "tensor", tensor, 2).astype(F32)
    s_out, s_up, s_down = second_grads[:, 0].T, second_grads[:, 1], second_grads[:, 2].T

    dq, dk, dv, q_sums = attend_back(
        queries, keys, values, attended, d_attended, lse, factor_pad, idr, idc
    )
    d_scale = jnp.sum(q_sums[:, 0, :HD], axis=0) / softplus * jax.nn.sigmoid(query_scale)

    def part(at):
        return sum(
            mm(lax.dynamic_slice(d, (at * rows, 0), (rows, d.shape[1])), w, 1, 1)
            for d, w in ((dq, wq), (dk, wk), (dv, wv))
        )

    far_same = part(order[1])
    far_other = part(order[3])
    near_same = part(order[0])
    near_other = part(order[2])
    from_x_same = swap(far_same.astype(BF), "tensor", tensor, 2).astype(F32)
    from_x_other = swap(far_other.astype(BF), "tensor", tensor, 2).astype(F32)
    chip_other = near_other + from_x_other
    d_normed = near_same + from_x_same + swap(chip_other.astype(BF), "tensor", tensor, 1).astype(F32)

    d_wq, d_wk, d_wv = (mm(normed, d, 0, 0) for d in (dq, dk, dv))
    w_dot = sum(
        jnp.sum(g * w.astype(F32), axis=1) for g, w in ((d_wq, wq), (d_wk, wk), (d_wv, wv))
    )
    late = jnp.concatenate([w_dot / attn_gain, jnp.pad(d_scale, (0, HP - HD))])
    late = sum_all(late.reshape(-1, HP), dp, tensor).reshape(-1)
    qkv_grad = jnp.concatenate([trim_heads(g) for g in (d_wq, d_wk, d_wv)], axis=1)
    s_qkv = scatter_dp(qkv_grad.reshape(dp, width // dp, 3 * cols), dp)

    d_tokens = (d_hidden + rms_back(d_normed, hat_one, inverse_one, attn_gain)).astype(BF)
    return (
        output,
        d_tokens,
        late[:width],
        s_qkv[:, :cols],
        s_qkv[:, cols : 2 * cols],
        s_qkv[:, 2 * cols :],
        late[width : width + HD],
        s_out,
        early[0],
        s_up,
        early[1],
        s_down,
        early[2],
    )


def solution(mesh):
    weight, turned, whole = P("dp", "tensor"), P("tensor", "dp"), P()
    positions = P(("dp", "tensor"), None)
    return jax.shard_map(
        lambda *args: body(mesh.shape["dp"], mesh.shape["tensor"], *args),
        mesh=mesh,
        in_specs=(positions, positions, P("dp", None), whole, weight, weight, weight, whole,
                  turned, whole, weight, whole, turned, whole),
        out_specs=(positions, positions, whole, weight, weight, weight, whole, turned, whole,
                   weight, whole, turned, whole),
        check_vma=False,
    )
```

time: 1200 us -> 608 us (0.51)
  waiting for transfers between devices: 501 us -> 174 us
  blocking collectives: 248 us -> 0 us
  matrix products: 264 us -> 88.5 us
  local copies, waits for them, and re-layouts: 67.5 us -> 175 us
  starting transfers between devices: 0.76 us -> 75.6 us
  other arithmetic: 94.6 us -> 30.3 us
  Pallas kernels: 0 us -> 52.4 us
  between operations: 14.7 us -> 2.09 us
    reduce_scatter x8 -> x0, waiting for transfers between devices: 285 us -> none  [the longest x1 70.1 us: body(): lax.psum_scatter(grad_query, 'dp', scatter_dimension=0, tiled=True)]
    all_gather x6 -> x0, blocking collectives: 207 us -> none  [the longest x1 35.3 us: body(): lax.all_gather(w_value, 'dp', axis=0, tiled=True)]
    dot_general x46 -> x27, matrix products: 264 us -> 88.5 us  [mm(): lax.dot_general(a, b, (((ca,), (cb,)), ((), ())), preferred_element_type=...]
    ppermute x0 -> x50, waiting for transfers between devices: none -> 174 us  [the longest x32 92.1 us: swap(): return lax.ppermute(v, axis, [(i, i ^ mask) for i in range(size)])]
    unnamed x16 -> x0, waiting for transfers between devices: 140 us -> none
    all_gather x4 -> x0, waiting for transfers between devices: 76.7 us -> none  [the longest x1 26.9 us: body(): lax.all_gather(full_up, 'tensor', axis=1, tiled=True)]
    ppermute x0 -> x50, starting transfers between devices: none -> 75.6 us  [the longest x32 30.3 us: swap(): return lax.ppermute(v, axis, [(i, i ^ mask) for i in range(size)])]
    concatenate x0 -> x11, local copies, waits for them, and re-layouts: none -> 62.3 us  [the longest x3 31.4 us: wide(): jnp.concatenate([half[:, at * cols:(at + 1) * cols], half[:, (3 + at) * c...]
  transfers between devices with their start and end apart: 14 -> 50, of which waited for: 11 -> 21; matrix products, arithmetic and copies ran while one was open for 24% -> 38% of each run, Pallas kernels for 0% -> 9%
where the time goes in v1:
time: 608 us; the launch traced here: 598 us
  local copies, waits for them, and re-layouts  175 us (29%)
  waiting for transfers between devices  174 us (29%)
  matrix products  88.5 us (15%)
  starting transfers between devices  75.6 us (12%)
  Pallas kernels  52.4 us (9%)
  other arithmetic  30.3 us (5%)
    ppermute x32, waiting for transfers between devices, swap(): return lax.ppermute(v, axis, [(i, i ^ mask) for i in range(size)])  92.1 us
    dot_general x27, matrix products, mm(): lax.dot_general(a, b, (((ca,), (cb,)), ((), ())), preferred_element_type=...  88.5 us
    ppermute x6, waiting for transfers between devices, scatter_dp(): lax.ppermute(piece.astype(BF), 'dp', [(i, (i + 2 * step) % size) for i in...  59.1 us
    pallas_call x1, Pallas kernels, attend_back(): pl.pallas_call(attend_back_kernel, grid=(heads,), out_shape=[jax.ShapeDty...  32.4 us
    concatenate x3, local copies, waits for them, and re-layouts, wide(): jnp.concatenate([half[:, at * cols:(at + 1) * cols], half[:, (3 + at) * c...  31.4 us
    ppermute x32, starting transfers between devices, swap(): return lax.ppermute(v, axis, [(i, i ^ mask) for i in range(size)])  30.3 us
    concatenate x6, local copies, waits for them, and re-layouts, body(): jnp.concatenate([trim_heads(g) for g in (d_wq, d_wk, d_wv)], axis=1)  28.7 us
    ppermute x6, starting transfers between devices, gather_dp(): lax.ppermute(shard, 'dp', [(i, (i + 2 * step) % size) for i in range(size)])  22.7 us
  transfers between devices with their start and end apart: 50, of which 21 were waited for; matrix products, arithmetic and copies ran while one was open for 38% of the time, Pallas kernels for 9%

profile of v1, /device:TPU:0, one launch (start us, length us, event | category | flops | bytes accessed | tf_op | source)
XLA Modules:
  0.0 597.9 jit_solution(16696474126916926971)
XLA Ops:
  18.5 28.1 %collective-permute-done.13 = bf16[160,960]{1,0:T(8,128)(2,1)} collective-permute-done((bf16[160,960]{1,0:T(8,128)(2,1)}, bf16[160,960]{1,0:T(8,128)(2,1)}, u32[]{:S(2)}, u32[]{:S(2)}) %collective-permute-start.13) | collective-permute-done | bytes 307232 | tf_op jit(solution)/shard_map/ppermute | solution.py:142
  74.1 11.6 %collective-permute-done.7 = bf16[160,960]{1,0:T(8,128)(2,1)S(1)} collective-permute-done((bf16[160,960]{1,0:T(8,128)(2,1)}, bf16[160,960]{1,0:T(8,128)(2,1)S(1)}, u32[]{:S(2)}, u32[]{:S(2)}) %collective-permute-start.7) | collective-permute-done | bytes 307232 | tf_op jit(solution)/shard_map/ppermute | solution.py:142
  87.3 5.5 collective-permute-done.9
  101.2 10.9 %collective-permute-start.19 = (bf16[160,1920]{1,0:T(8,128)(2,1)}, bf16[160,1920]{1,0:T(8,128)(2,1)S(1)}, u32[]{:S(2)}, u32[]{:S(2)}) collective-permute-start(bf16[160,1920]{1,0:T(8,128)(2,1)} %concatenate.48), channel_id=1, source_target_pairs={{0,24},{4,28},{8,0},{12,4},{16,8},{20,12},{24,16},{28,20},{1,25},{... | collective-permute-start | bytes 1843208 | tf_op jit(solution)/shard_map/ppermute | solution.py:153
  135.3 6.9 %collective-permute-done.18 = bf16[160,1920]{1,0:T(8,128)(2,1)S(1)} collective-permute-done((bf16[160,1920]{1,0:T(8,128)(2,1)}, bf16[160,1920]{1,0:T(8,128)(2,1)S(1)}, u32[]{:S(2)}, u32[]{:S(2)}) %collective-permute-start.18) | collective-permute-done | bytes 614432 | tf_op jit(solution)/shard_map/ppermute | solution.py:142
  144.0 8.3 %collective-permute-done.20 = bf16[160,1920]{1,0:T(8,128)(2,1)S(1)} collective-permute-done((bf16[160,1920]{1,0:T(8,128)(2,1)S(1)}, bf16[160,1920]{1,0:T(8,128)(2,1)S(1)}, u32[]{:S(2)}, u32[]{:S(2)}) %collective-permute-start.20) | collective-permute-done | bytes 614432 | tf_op jit(solution)/shard_map/ppermute | solution.py:142
  153.3 7.3 %fusion.72 = (bf16[1280,320]{1,0:T(8,128)(2,1)}, bf16[1280,320]{1,0:T(8,128)(2,1)}, bf16[1280,320]{1,0:T(8,128)(2,1)}, bf16[1280,320]{1,0:T(8,128)(2,1)}, bf16[1...) fusion(bf16[1280,1920]{1,0:T(8,128)(2,1)} %bitcast.29), kind=kLoop, calls=%fused_computation.186 | loop fusion | bytes 9830400 | tf_op jit(solution)/shard_map/slice | solution.py:248
  173.7 20.0 %shard_map.237 = (bf16[2048,512]{1,0:T(8,128)(2,1)}, f32[4,1,2048]{2,1,0:T(1,128)}) custom-call(bf16[2048,512]{1,0:T(8,128)(2,1)} %multiply_convert_fusion.q_ref, bf16[2048,512]{1,0:T(8,128)(2,1)} %convolution_convert_fusion.2.k_ref, bf16[2048,512]{1,0:T(8,128)(2,1)} %convolution_convert_fusion.1.v_ref, s32[1,2048]{1,0:T(1,128)} %idr_ref.3, ...), custom_call_target="tpu_custom_call" | custom-call | flops 17179869184 | bytes 8388608 | tf_op jit(solution)/shard_map/pallas_call | solution.py:60
  202.3 7.1 %fusion.71 = (bf16[1280,320]{1,0:T(8,128)(2,1)}, bf16[1280,320]{1,0:T(8,128)(2,1)}, bf16[1280,320]{1,0:T(8,128)(2,1)}, bf16[1280,320]{1,0:T(8,128)(2,1)}, bf16[1...) fusion(bf16[1280,1920]{1,0:T(8,128)(2,1)} %collective-permute-done.21), kind=kLoop, calls=%fused_computation.185 | loop fusion | bytes 9830400 | tf_op jit(solution)/shard_map/slice | solution.py:250
  209.4 17.9 %concatenate.49 = bf16[1280,1280]{1,0:T(8,128)(2,1)} concatenate(bf16[1280,320]{1,0:T(8,128)(2,1)} %get-tuple-element.65, bf16[1280,320]{1,0:T(8,128)(2,1)} %get-tuple-element.64, bf16[1280,320]{1,0:T(8,128)(2,1)} %get-tuple-element.59, bf16[1280,320]{1,0:T(8,128)(2,1)} %get-tuple-element.58), dimensions={1} | concatenate | bytes 6553600 | tf_op jit(solution)/shard_map/concatenate | solution.py:245
  227.3 6.2 %multiply_reduce_fusion.5 = (f32[512]{0:T(512)S(1)}, f32[512,1280]{1,0:T(8,128)}) fusion(bf16[1280,1280]{1,0:T(8,128)(2,1)} %concatenate.49, bf16[512,320]{0,1:T(8,128)(2,1)} %collective-permute-done.12, bf16[512,320]{0,1:T(8,128)(2,1)} %collective-permute-done.11, bf16[512,320]{0,1:T(8,128)(2,1)} %collective-permute-done.10, ...), kind=kOutput, calls=%fused_computation.59 | convolution fusion | flops 1685585408 | bytes 8521728 | tf_op jit(solution)/shard_map/dot_general | solution.py:22
  233.4 6.7 %concatenate.50 = bf16[1280,1280]{1,0:T(8,128)(2,1)} concatenate(bf16[1280,320]{1,0:T(8,128)(2,1)} %get-tuple-element.63, bf16[1280,320]{1,0:T(8,128)(2,1)} %get-tuple-element.60, bf16[1280,320]{1,0:T(8,128)(2,1)} %get-tuple-element.57, bf16[1280,320]{1,0:T(8,128)(2,1)} %get-tuple-element.54), dimensions={1} | concatenate | bytes 6553600 | tf_op jit(solution)/shard_map/concatenate | solution.py:245
  240.2 4.7 convolution_add_fusion.9
  245.0 4.6 convolution_bitcast_fusion
  249.6 6.8 %concatenate.52 = bf16[1280,1280]{1,0:T(8,128)(2,1)} concatenate(bf16[1280,320]{1,0:T(8,128)(2,1)} %get-tuple-element.62, bf16[1280,320]{1,0:T(8,128)(2,1)} %get-tuple-element.61, bf16[1280,320]{1,0:T(8,128)(2,1)} %get-tuple-element.56, bf16[1280,320]{1,0:T(8,128)(2,1)} %get-tuple-element.55), dimensions={1} | concatenate | bytes 6553600 | tf_op jit(solution)/shard_map/concatenate | solution.py:245
  256.4 5.6 convert_reduce_fusion.1
  264.1 4.8 fusion.69
  297.3 4.9 pad_maximum_fusion.1
  302.3 8.6 %collective-permute-start.47 = (f32[3,1280]{1,0:T(4,128)S(1)}, f32[3,1280]{1,0:T(4,128)S(1)}, u32[]{:S(2)}, u32[]{:S(2)}) collective-permute-start(f32[3,1280]{1,0:T(4,128)S(1)} %get-tuple-element.44), channel_id=1, source_target_pairs={{0,8},{4,12},{8,16},{12,20},{16,24},{20,28},{24,0},{28,4},{1,9},{5... | collective-permute-start | bytes 46088 | tf_op jit(solution)/shard_map/ppermute | solution.py:188
  337.2 32.4 %shard_map.238 = (bf16[2048,512]{1,0:T(8,128)(2,1)}, bf16[2048,512]{1,0:T(8,128)(2,1)}, bf16[2048,512]{1,0:T(8,128)(2,1)}, f32[4,1,128]{2,1,0:T(1,128)}) custom-call(bf16[2048,512]{1,0:T(8,128)(2,1)} %multiply_convert_fusion.q_ref, bf16[2048,512]{1,0:T(8,128)(2,1)} %convolution_convert_fusion.2.k_ref, bf16[2048,512]{1,0:T(8,128)(2,1)} %convolution_convert_fusion.1.v_ref, ...), custom_call_target="tpu_custom_call" | custom-call | flops 34359738368 | bytes 16777216 | tf_op jit(solution)/shard_map/pallas_call | solution.py:120
  371.7 7.8 %multiply_reduce_fusion.3 = (f32[1280]{0:T(1024)S(1)}, f32[1280,512]{0,1:T(8,128)}) fusion(bf16[1280,4,128]{0,2,1:T(8,128)(2,1)S(1)} %copy-done.1, bf16[2048,1280]{1,0:T(8,128)(2,1)} %copy-done.11, bf16[2048,512]{1,0:T(8,128)(2,1)} %get-tuple-element.21), kind=kOutput, calls=%fused_computation.52 | convolution fusion | flops 2686319360 | bytes 11277312 | tf_op jit(solution)/shard_map/dot_general | solution.py:22
  403.6 5.0 concatenate.56
  414.5 6.1 %concatenate.55 = f32[4,2,160,320]{2,1,0,3:T(2,128)} reshape(f32[1280,4,80]{0,2,1:T(8,128)} %slice.258) | data formatting | bytes 3276800 | tf_op jit(solution)/shard_map/concatenate | solution.py:352
  427.7 6.1 %concatenate.54 = f32[4,2,160,320]{2,1,0,3:T(2,128)} reshape(f32[1280,4,80]{0,2,1:T(8,128)} %slice.257) | data formatting | bytes 3276800 | tf_op jit(solution)/shard_map/concatenate | solution.py:352
  454.4 6.3 %maximum_add_fusion = f32[1280,1920]{0,1:T(8,128)} fusion(f32[1280,640]{0,1:T(8,128)S(1)} %slice-done.6, f32[1280,640]{0,1:T(8,128)S(1)} %slice-done.5, f32[1280,640]{0,1:T(8,128)S(1)} %slice-done.7, bf16[1280,1920]{0,1:T(8,128)(2,1)} %collective-permute-done.38), kind=kLoop, calls=%fused_computation | loop fusion | flops 9830400 | bytes 24576000 | tf_op jit(solution)/shard_map/add | solution.py:320
  460.6 11.1 %copy.93 = f32[1280,1920]{1,0:T(8,128)} copy(f32[1280,1920]{0,1:T(8,128)} %maximum_add_fusion) | data formatting | bytes 19660800 | tf_op jit(solution)/shard_map/add | solution.py:320
  490.8 5.1 collective-permute-done.37
  495.8 11.0 %collective-permute-done.36 = bf16[160,960]{1,0:T(8,128)(2,1)S(1)} collective-permute-done((bf16[160,960]{1,0:T(8,128)(2,1)S(1)}, bf16[160,960]{1,0:T(8,128)(2,1)S(1)}, u32[]{:S(2)}, u32[]{:S(2)}) %collective-permute-start.36) | collective-permute-done | bytes 307232 | tf_op jit(solution)/shard_map/ppermute | solution.py:176
  508.0 21.6 %collective-permute-done.39 = bf16[4,160,1920]{2,1,0:T(8,128)(2,1)S(1)} collective-permute-done((bf16[4,160,1920]{2,1,0:T(8,128)(2,1)S(1)}, bf16[4,160,1920]{2,1,0:T(8,128)(2,1)S(1)}, u32[]{:S(2)}, u32[]{:S(2)}) %collective-permute-start.39) | collective-permute-done | bytes 2457632 | tf_op jit(solution)/shard_map/ppermute | solution.py:142
  539.1 9.0 %collective-permute-done.42 = bf16[160,1920]{1,0:T(8,128)(2,1)S(1)} collective-permute-done((bf16[160,1920]{1,0:T(8,128)(2,1)S(1)}, bf16[160,1920]{1,0:T(8,128)(2,1)S(1)}, u32[]{:S(2)}, u32[]{:S(2)}) %collective-permute-start.42) | collective-permute-done | bytes 614432 | tf_op jit(solution)/shard_map/ppermute | solution.py:176
  548.1 33.9 %collective-permute-done.41 = bf16[160,1920]{1,0:T(8,128)(2,1)S(1)} collective-permute-done((bf16[160,1920]{1,0:T(8,128)(2,1)S(1)}, bf16[160,1920]{1,0:T(8,128)(2,1)S(1)}, u32[]{:S(2)}, u32[]{:S(2)}) %collective-permute-start.41) | collective-permute-done | bytes 614432 | tf_op jit(solution)/shard_map/ppermute | solution.py:176
  590.0 5.0 fusion.15
  (345 shorter events, 258.8 us)
Async XLA Ops:
  7.4 120.1 %collective-permute-start = (bf16[512,1280]{1,0:T(8,128)(2,1)}, bf16[512,1280]{1,0:T(8,128)(2,1)}, u32[]{:S(2)}, u32[]{:S(2)}) collective-permute-start(bf16[512,1280]{1,0:T(8,128)(2,1)} %get-tuple-element.50), channel_id=1, source_target_pairs={{0,2},{1,3},{2,0},{3,1},{4,6},{5,7},{6,4},{7,5},{8,10},{9,11},{10,... | collective-permute-start | bytes 3932168 | tf_op jit(solution)/shard_map/ppermute | solution.py:142
  10.4 119.6 %collective-permute-start.1 = (bf16[512,1280]{1,0:T(8,128)(2,1)}, bf16[512,1280]{1,0:T(8,128)(2,1)}, u32[]{:S(2)}, u32[]{:S(2)}) collective-permute-start(bf16[512,1280]{1,0:T(8,128)(2,1)} %get-tuple-element.50), channel_id=1, source_target_pairs={{0,1},{1,0},{2,3},{3,2},{4,5},{5,4},{6,7},{7,6},{8,9},{9,8},{10,11... | collective-permute-start | bytes 3932168 | tf_op jit(solution)/shard_map/ppermute | solution.py:142
  11.9 44.0 %collective-permute-start.3 = (bf16[160,960]{1,0:T(8,128)(2,1)S(1)}, bf16[160,960]{1,0:T(8,128)(2,1)}, u32[]{:S(2)}, u32[]{:S(2)}) collective-permute-start(bf16[160,960]{1,0:T(8,128)(2,1)S(1)} %get-tuple-element.48), channel_id=1, source_target_pairs={{0,4},{4,0},{8,12},{12,8},{16,20},{20,16},{24,28},{28,24},{1,5},{5... | collective-permute-start | bytes 921608 | tf_op jit(solution)/shard_map/ppermute | solution.py:142
  13.4 43.8 %collective-permute-start.4 = (bf16[160,960]{1,0:T(8,128)(2,1)S(1)}, bf16[160,960]{1,0:T(8,128)(2,1)}, u32[]{:S(2)}, u32[]{:S(2)}) collective-permute-start(bf16[160,960]{1,0:T(8,128)(2,1)S(1)} %get-tuple-element.48), channel_id=1, source_target_pairs={{0,8},{4,12},{8,16},{12,20},{16,24},{20,28},{24,0},{28,4},{1,9},{5... | collective-permute-start | bytes 921608 | tf_op jit(solution)/shard_map/ppermute | solution.py:153
  15.9 30.7 %collective-permute-start.13 = (bf16[160,960]{1,0:T(8,128)(2,1)}, bf16[160,960]{1,0:T(8,128)(2,1)}, u32[]{:S(2)}, u32[]{:S(2)}) collective-permute-start(bf16[160,960]{1,0:T(8,128)(2,1)} %pad_maximum_fusion.4), channel_id=1, source_target_pairs={{0,2},{1,3},{2,0},{3,1},{4,6},{5,7},{6,4},{7,5},{8,10},{9,11},{10,... | collective-permute-start | bytes 921608 | tf_op jit(solution)/shard_map/ppermute | solution.py:142
  64.6 36.6 %collective-permute-start.14 = (bf16[160,1920]{1,0:T(8,128)(2,1)}, bf16[160,1920]{1,0:T(8,128)(2,1)}, u32[]{:S(2)}, u32[]{:S(2)}) collective-permute-start(bf16[160,1920]{1,0:T(8,128)(2,1)} %concatenate.48), channel_id=1, source_target_pairs={{0,4},{4,0},{8,12},{12,8},{16,20},{20,16},{24,28},{28,24},{1,5},{5... | collective-permute-start | bytes 1843208 | tf_op jit(solution)/shard_map/ppermute | solution.py:142
  66.1 19.6 %collective-permute-start.7 = (bf16[160,960]{1,0:T(8,128)(2,1)}, bf16[160,960]{1,0:T(8,128)(2,1)S(1)}, u32[]{:S(2)}, u32[]{:S(2)}) collective-permute-start(bf16[160,960]{1,0:T(8,128)(2,1)} %collective-permute-done.6), channel_id=1, source_target_pairs={{0,4},{4,0},{8,12},{12,8},{16,20},{20,16},{24,28},{28,24},{1,5},{5... | collective-permute-start | bytes 921608 | tf_op jit(solution)/shard_map/ppermute | solution.py:142
  70.2 41.9 %collective-permute-start.15 = (bf16[160,1920]{1,0:T(8,128)(2,1)}, bf16[160,1920]{1,0:T(8,128)(2,1)}, u32[]{:S(2)}, u32[]{:S(2)}) collective-permute-start(bf16[160,1920]{1,0:T(8,128)(2,1)} %concatenate.48), channel_id=1, source_target_pairs={{0,8},{4,12},{8,16},{12,20},{16,24},{20,28},{24,0},{28,4},{1,9},{5... | collective-permute-start | bytes 1843208 | tf_op jit(solution)/shard_map/ppermute | solution.py:153
  92.8 27.7 %collective-permute-start.17 = (bf16[160,1920]{1,0:T(8,128)(2,1)}, bf16[160,1920]{1,0:T(8,128)(2,1)}, u32[]{:S(2)}, u32[]{:S(2)}) collective-permute-start(bf16[160,1920]{1,0:T(8,128)(2,1)} %concatenate.48), channel_id=1, source_target_pairs={{0,16},{4,20},{8,24},{12,28},{16,0},{20,4},{24,8},{28,12},{1,17},{... | collective-permute-start | bytes 1843208 | tf_op jit(solution)/shard_map/ppermute | solution.py:153
  101.2 24.9 %collective-permute-start.19 = (bf16[160,1920]{1,0:T(8,128)(2,1)}, bf16[160,1920]{1,0:T(8,128)(2,1)S(1)}, u32[]{:S(2)}, u32[]{:S(2)}) collective-permute-start(bf16[160,1920]{1,0:T(8,128)(2,1)} %concatenate.48), channel_id=1, source_target_pairs={{0,24},{4,28},{8,0},{12,4},{16,8},{20,12},{24,16},{28,20},{1,25},{... | collective-permute-start | bytes 1843208 | tf_op jit(solution)/shard_map/ppermute | solution.py:153
  112.1 20.4 %collective-permute-start.16 = (bf16[160,1920]{1,0:T(8,128)(2,1)}, bf16[160,1920]{1,0:T(8,128)(2,1)S(1)}, u32[]{:S(2)}, u32[]{:S(2)}) collective-permute-start(bf16[160,1920]{1,0:T(8,128)(2,1)} %collective-permute-done.15), channel_id=1, source_target_pairs={{0,4},{4,0},{8,12},{12,8},{16,20},{20,16},{24,28},{28,24},{1,5},{5... | collective-permute-start | bytes 1843208 | tf_op jit(solution)/shard_map/ppermute | solution.py:142
  120.6 21.7 %collective-permute-start.18 = (bf16[160,1920]{1,0:T(8,128)(2,1)}, bf16[160,1920]{1,0:T(8,128)(2,1)S(1)}, u32[]{:S(2)}, u32[]{:S(2)}) collective-permute-start(bf16[160,1920]{1,0:T(8,128)(2,1)} %collective-permute-done.17), channel_id=1, source_target_pairs={{0,4},{4,0},{8,12},{12,8},{16,20},{20,16},{24,28},{28,24},{1,5},{5... | collective-permute-start | bytes 1843208 | tf_op jit(solution)/shard_map/ppermute | solution.py:142
  126.0 26.3 %collective-permute-start.20 = (bf16[160,1920]{1,0:T(8,128)(2,1)S(1)}, bf16[160,1920]{1,0:T(8,128)(2,1)S(1)}, u32[]{:S(2)}, u32[]{:S(2)}) collective-permute-start(bf16[160,1920]{1,0:T(8,128)(2,1)S(1)} %collective-permute-done.19), channel_id=1, source_target_pairs={{0,4},{4,0},{8,12},{12,8},{16,20},{20,16},{24,28},{28,24},{1,5},{5... | collective-permute-start | bytes 1843208 | tf_op jit(solution)/shard_map/ppermute | solution.py:142
  127.6 33.0 %collective-permute-start.2 = (bf16[512,1280]{1,0:T(8,128)(2,1)}, bf16[512,1280]{1,0:T(8,128)(2,1)S(1)}, u32[]{:S(2)}, u32[]{:S(2)}) collective-permute-start(bf16[512,1280]{1,0:T(8,128)(2,1)} %collective-permute-done), channel_id=1, source_target_pairs={{0,1},{1,0},{2,3},{3,2},{4,5},{5,4},{6,7},{7,6},{8,9},{9,8},{10,11... | collective-permute-start | bytes 3932168 | tf_op jit(solution)/shard_map/ppermute | solution.py:142
  153.3 49.0 %collective-permute-start.21 = (bf16[1280,1920]{1,0:T(8,128)(2,1)}, bf16[1280,1920]{1,0:T(8,128)(2,1)}, u32[]{:S(2)}, u32[]{:S(2)}) collective-permute-start(bf16[1280,1920]{1,0:T(8,128)(2,1)} %bitcast.29), channel_id=1, source_target_pairs={{0,1},{1,0},{2,3},{3,2},{4,5},{5,4},{6,7},{7,6},{8,9},{9,8},{10,11... | collective-permute-start | bytes 14745608 | tf_op jit(solution)/shard_map/ppermute | solution.py:142
  200.1 27.1 %collective-permute-start.12 = (bf16[512,320]{0,1:T(8,128)(2,1)}, bf16[512,320]{0,1:T(8,128)(2,1)}, u32[]{:S(2)}, u32[]{:S(2)}) collective-permute-start(bf16[512,320]{0,1:T(8,128)(2,1)} %get-tuple-element.79), channel_id=1, source_target_pairs={{0,3},{1,2},{2,1},{3,0},{4,7},{5,6},{6,5},{7,4},{8,11},{9,10},{10,... | collective-permute-start | bytes 983048 | tf_op jit(solution)/shard_map/ppermute | solution.py:142
  201.6 25.7 %collective-permute-start.11 = (bf16[512,320]{0,1:T(8,128)(2,1)}, bf16[512,320]{0,1:T(8,128)(2,1)}, u32[]{:S(2)}, u32[]{:S(2)}) collective-permute-start(bf16[512,320]{0,1:T(8,128)(2,1)} %get-tuple-element.80), channel_id=1, source_target_pairs={{0,1},{1,0},{2,3},{3,2},{4,5},{5,4},{6,7},{7,6},{8,9},{9,8},{10,11... | collective-permute-start | bytes 983048 | tf_op jit(solution)/shard_map/ppermute | solution.py:142
  201.7 25.5 %collective-permute-start.10 = (bf16[512,320]{0,1:T(8,128)(2,1)S(1)}, bf16[512,320]{0,1:T(8,128)(2,1)}, u32[]{:S(2)}, u32[]{:S(2)}) collective-permute-start(bf16[512,320]{0,1:T(8,128)(2,1)S(1)} %get-tuple-element.81), channel_id=1, source_target_pairs={{0,2},{1,3},{2,0},{3,1},{4,6},{5,7},{6,4},{7,5},{8,10},{9,11},{10,... | collective-permute-start | bytes 983048 | tf_op jit(solution)/shard_map/ppermute | solution.py:142
  293.4 31.2 %collective-permute-start.22 = (bf16[512,320]{1,0:T(8,128)(2,1)}, bf16[512,320]{1,0:T(8,128)(2,1)}, u32[]{:S(2)}, u32[]{:S(2)}) collective-permute-start(bf16[512,320]{1,0:T(8,128)(2,1)} %get-tuple-element.76), channel_id=1, source_target_pairs={{0,2},{1,3},{2,0},{3,1},{4,6},{5,7},{6,4},{7,5},{8,10},{9,11},{10,... | collective-permute-start | bytes 983048 | tf_op jit(solution)/shard_map/ppermute | solution.py:142
  294.4 31.3 %collective-permute-start.23 = (bf16[512,320]{1,0:T(8,128)(2,1)}, bf16[512,320]{1,0:T(8,128)(2,1)}, u32[]{:S(2)}, u32[]{:S(2)}) collective-permute-start(bf16[512,320]{1,0:T(8,128)(2,1)} %get-tuple-element.75), channel_id=1, source_target_pairs={{0,1},{1,0},{2,3},{3,2},{4,5},{5,4},{6,7},{7,6},{8,9},{9,8},{10,11... | collective-permute-start | bytes 983048 | tf_op jit(solution)/shard_map/ppermute | solution.py:142
  294.6 33.8 %collective-permute-start.24 = (bf16[512,320]{1,0:T(8,128)(2,1)}, bf16[512,320]{1,0:T(8,128)(2,1)}, u32[]{:S(2)}, u32[]{:S(2)}) collective-permute-start(bf16[512,320]{1,0:T(8,128)(2,1)} %get-tuple-element.74), channel_id=1, source_target_pairs={{0,3},{1,2},{2,1},{3,0},{4,7},{5,6},{6,5},{7,4},{8,11},{9,10},{10,... | collective-permute-start | bytes 983048 | tf_op jit(solution)/shard_map/ppermute | solution.py:142
  302.2 150.1 %collective-permute-start.38 = (bf16[1280,1920]{0,1:T(8,128)(2,1)}, bf16[1280,1920]{0,1:T(8,128)(2,1)}, u32[]{:S(2)}, u32[]{:S(2)}) collective-permute-start(bf16[1280,1920]{0,1:T(8,128)(2,1)} %pad_maximum_fusion.1), channel_id=1, source_target_pairs={{0,1},{1,0},{2,3},{3,2},{4,5},{5,4},{6,7},{7,6},{8,9},{9,8},{10,11... | collective-permute-start | bytes 14745608 | tf_op jit(solution)/shard_map/ppermute | solution.py:142
  385.4 102.5 %collective-permute-start.26 = (bf16[512,1280]{1,0:T(8,128)(2,1)}, bf16[512,1280]{1,0:T(8,128)(2,1)}, u32[]{:S(2)}, u32[]{:S(2)}) collective-permute-start(bf16[512,1280]{1,0:T(8,128)(2,1)} %fusion.9), channel_id=1, source_target_pairs={{0,2},{1,3},{2,0},{3,1},{4,6},{5,7},{6,4},{7,5},{8,10},{9,11},{10,... | collective-permute-start | bytes 3932168 | tf_op jit(solution)/shard_map/ppermute | solution.py:142
  399.1 135.4 %collective-permute-start.25 = (bf16[512,1280]{1,0:T(8,128)(2,1)}, bf16[512,1280]{1,0:T(8,128)(2,1)}, u32[]{:S(2)}, u32[]{:S(2)}) collective-permute-start(bf16[512,1280]{1,0:T(8,128)(2,1)} %fusion.8), channel_id=1, source_target_pairs={{0,2},{1,3},{2,0},{3,1},{4,6},{5,7},{6,4},{7,5},{8,10},{9,11},{10,... | collective-permute-start | bytes 3932168 | tf_op jit(solution)/shard_map/ppermute | solution.py:142
  400.1 42.2 %collective-permute-start.29 = (f32[11,128]{1,0:T(8,128)S(1)}, f32[11,128]{1,0:T(8,128)S(1)}, u32[]{:S(2)}, u32[]{:S(2)}) collective-permute-start(f32[11,128]{1,0:T(8,128)S(1)} %fusion.114), channel_id=1, source_target_pairs={{0,2},{1,3},{2,0},{3,1},{4,6},{5,7},{6,4},{7,5},{8,10},{9,11},{10,... | collective-permute-start | bytes 16904 | tf_op jit(solution)/shard_map/ppermute | solution.py:142
  449.5 31.2 %collective-permute-start.34 = (bf16[4,160,960]{2,1,0:T(8,128)(2,1)S(1)}, bf16[4,160,960]{2,1,0:T(8,128)(2,1)}, u32[]{:S(2)}, u32[]{:S(2)}) collective-permute-start(bf16[4,160,960]{2,1,0:T(8,128)(2,1)S(1)} %fusion.18), channel_id=1, source_target_pairs={{0,4},{4,0},{8,12},{12,8},{16,20},{20,16},{24,28},{28,24},{1,5},{5... | collective-permute-start | bytes 3686408 | tf_op jit(solution)/shard_map/ppermute | solution.py:142
  452.2 22.3 %collective-permute-start.32 = (f32[11,128]{1,0:T(8,128)S(1)}, f32[11,128]{1,0:T(8,128)S(1)}, u32[]{:S(2)}, u32[]{:S(2)}) collective-permute-start(f32[11,128]{1,0:T(8,128)S(1)} %get-tuple-element.46), channel_id=1, source_target_pairs={{0,16},{4,20},{8,24},{12,28},{16,0},{20,4},{24,8},{28,12},{1,17},{... | collective-permute-start | bytes 16904 | tf_op jit(solution)/shard_map/ppermute | solution.py:188
  452.4 23.2 %collective-permute-start.33 = (f32[11,128]{1,0:T(8,128)S(1)}, f32[11,128]{1,0:T(8,128)S(1)}, u32[]{:S(2)}, u32[]{:S(2)}) collective-permute-start(f32[11,128]{1,0:T(8,128)S(1)} %get-tuple-element.46), channel_id=1, source_target_pairs={{0,24},{4,28},{8,0},{12,4},{16,8},{20,12},{24,16},{28,20},{1,25},{... | collective-permute-start | bytes 16904 | tf_op jit(solution)/shard_map/ppermute | solution.py:188
  474.6 55.0 %collective-permute-start.39 = (bf16[4,160,1920]{2,1,0:T(8,128)(2,1)S(1)}, bf16[4,160,1920]{2,1,0:T(8,128)(2,1)S(1)}, u32[]{:S(2)}, u32[]{:S(2)}) collective-permute-start(bf16[4,160,1920]{2,1,0:T(8,128)(2,1)S(1)} %fusion.17), channel_id=1, source_target_pairs={{0,4},{4,0},{8,12},{12,8},{16,20},{20,16},{24,28},{28,24},{1,5},{5... | collective-permute-start | bytes 7372808 | tf_op jit(solution)/shard_map/ppermute | solution.py:142
  495.8 38.6 %collective-permute-start.27 = (bf16[512,1280]{1,0:T(8,128)(2,1)S(1)}, bf16[512,1280]{1,0:T(8,128)(2,1)S(1)}, u32[]{:S(2)}, u32[]{:S(2)}) collective-permute-start(bf16[512,1280]{1,0:T(8,128)(2,1)S(1)} %add_convert_fusion), channel_id=1, source_target_pairs={{0,1},{1,0},{2,3},{3,2},{4,5},{5,4},{6,7},{7,6},{8,9},{9,8},{10,11... | collective-permute-start | bytes 3932168 | tf_op jit(solution)/shard_map/ppermute | solution.py:142
  533.8 48.3 %collective-permute-start.41 = (bf16[160,1920]{1,0:T(8,128)(2,1)S(1)}, bf16[160,1920]{1,0:T(8,128)(2,1)S(1)}, u32[]{:S(2)}, u32[]{:S(2)}) collective-permute-start(bf16[160,1920]{1,0:T(8,128)(2,1)S(1)} %get-tuple-element.53), channel_id=1, source_target_pairs={{0,16},{4,20},{8,24},{12,28},{16,0},{20,4},{24,8},{28,12},{1,17},{... | collective-permute-start | bytes 1843208 | tf_op jit(solution)/shard_map/ppermute | solution.py:176
  533.8 48.3 %collective-permute-start.40 = (bf16[160,1920]{1,0:T(8,128)(2,1)S(1)}, bf16[160,1920]{1,0:T(8,128)(2,1)S(1)}, u32[]{:S(2)}, u32[]{:S(2)}) collective-permute-start(bf16[160,1920]{1,0:T(8,128)(2,1)S(1)} %get-tuple-element.51), channel_id=1, source_target_pairs={{0,8},{4,12},{8,16},{12,20},{16,24},{20,28},{24,0},{28,4},{1,9},{5... | collective-permute-start | bytes 1843208 | tf_op jit(solution)/shard_map/ppermute | solution.py:176
  (74 other events, 666.0 us)

commit v2 on v1

--- a/solution.py
+++ b/solution.py
@@ -26,64 +26,11 @@
     return min((tile + 1) * TILE + BLOCK_MOST, length)
 
 
-def attend_kernel(q_ref, k_ref, v_ref, idr_ref, idc_ref, o_ref, lse_ref, vt_ref):
-    length = q_ref.shape[0]
-    tiles = length // TILE
-    sub = lax.broadcasted_iota(jnp.int32, (HP, length), 0)
-    vt_ref[...] = jnp.where(sub == HD, 1.0, v_ref[...].astype(F32).T).astype(BF)
-
-    def scores(t):
-        seen, low = reach(t, length), t * TILE
-        st = mm(k_ref[:seen, :], q_ref[low : low + TILE, :], 1, 1)
-        visible = idc_ref[low:seen, :] <= idr_ref[:, low : low + TILE]
-        masked = jnp.where(visible, st[low:], MASKED)
-        return jnp.concatenate([st[:low], masked], 0) if low else masked
-
-    st = scores(0)
-    for t in range(tiles):
-        later = scores(t + 1) if t + 1 < tiles else None
-        seen, low = st.shape[0], t * TILE
-        group = jnp.max(st.reshape(seen // 64, 64, TILE), axis=0)
-        highest = jnp.max(group, axis=0, keepdims=True)
-        weights = jnp.exp(st - highest).astype(BF)
-        ot = mm(vt_ref[:, :seen], weights, 1, 0)
-        summed = ot[HD : HD + 1, :]
-        o_ref[low : low + TILE, :] = (ot * (1.0 / summed)).T.astype(BF)
-        lse_ref[0, :, low : low + TILE] = highest + jnp.log(summed)
-        st = later
-
-
-def attend(q, k, v, idr, idc):
-    length, wide = q.shape
-    heads = wide // HP
-    col = pl.BlockSpec((length, HP), lambda h: (0, h))
-    return pl.pallas_call(
-        attend_kernel,
-        grid=(heads,),
-        out_shape=[
-            jax.ShapeDtypeStruct((length, wide), BF),
-            jax.ShapeDtypeStruct((heads, 1, length), F32),
-        ],
-        in_specs=[
-            col,
-            col,
-            col,
-            pl.BlockSpec((1, length), lambda h: (0, 0)),
-            pl.BlockSpec((length, 1), lambda h: (0, 0)),
-        ],
-        out_specs=[col, pl.BlockSpec((1, 1, length), lambda h: (h, 0, 0))],
-        scratch_shapes=[pltpu.VMEM((HP, length), BF)],
-        compiler_params=pltpu.CompilerParams(vmem_limit_bytes=56 << 20),
-        cost_estimate=pl.CostEstimate(
-            flops=heads * length * length * 2 * 256 * 2, bytes_accessed=8 << 20, transcendentals=0
-        ),
-    )(q, k, v, idr, idc)
-
-
 def attend_back_kernel(
     q_ref, k_ref, v_ref, o_ref, do_ref, lse_ref, fac_ref, idr_ref, idc_ref,
     dq_ref, dk_ref, dv_ref, qs_ref, dka, dva, kt_ref,
 ):
+    q_ref, k_ref, v_ref = q_ref.at[0], k_ref.at[0], v_ref.at[0]
     length = q_ref.shape[0]
     tiles = length // TILE
     kt_ref[...] = k_ref[...].astype(F32).T.astype(BF)
@@ -95,7 +42,9 @@
         rows = slice(low, low + TILE)
         qt = q_ref[rows, :]
         dot_ = do_ref[rows, :]
-        delta = jnp.sum((dot_.astype(F32) * o_ref[rows, :].astype(F32)).T, axis=0, keepdims=True)
+        delta = jnp.sum(
+            dot_.astype(F32).T[:HD] * o_ref[0, :, rows].astype(F32), axis=0, keepdims=True
+        )
         st = mm(k_ref[:seen, :], qt, 1, 1)
         p = jnp.exp(st - lse_ref[0, :, rows])
         visible = idc_ref[low:seen, :] <= idr_ref[:, rows]
@@ -114,16 +63,17 @@
 
 
 def attend_back(q, k, v, o, do, lse, factor, idr, idc):
-    length, wide = q.shape
-    heads = wide // HP
+    heads, length, _ = q.shape
+    wide = heads * HP
     col = pl.BlockSpec((length, HP), lambda h: (0, h))
+    head = pl.BlockSpec((1, length, HP), lambda h: (h, 0, 0))
     return pl.pallas_call(
         attend_back_kernel,
         grid=(heads,),
         out_shape=[jax.ShapeDtypeStruct((length, wide), BF)] * 3
         + [jax.ShapeDtypeStruct((heads, 1, HP), F32)],
         in_specs=[
-            col, col, col, col, col,
+            head, head, head, pl.BlockSpec((1, HD, length), lambda h: (h, 0, 0)), col,
             pl.BlockSpec((1, 1, length), lambda h: (h, 0, 0)),
             pl.BlockSpec((1, HP), lambda h: (0, 0)),
             pl.BlockSpec((1, length), lambda h: (0, 0)),
@@ -136,6 +86,345 @@
             flops=heads * length * length * 2 * 256 * 4, bytes_accessed=16 << 20, transcendentals=0
         ),
     )(q, k, v, o, do, lse, factor, idr, idc)
+
+
+MESH = pl.DeviceIdType.MESH
+PARTNERS = (2, 1, 3)
+SLOT = {0: 0, 2: 1, 1: 2, 3: 3}
+
+
+def remote(src, dst, send, recv, where):
+    return pltpu.make_async_remote_copy(
+        src_ref=src, dst_ref=dst, send_sem=send, recv_sem=recv, device_id=where, device_id_type=MESH
+    )
+
+
+def greet(peers):
+    barrier = pltpu.get_barrier_semaphore()
+    for where in peers:
+        pl.semaphore_signal(barrier, inc=1, device_id=where, device_id_type=MESH)
+    pl.semaphore_wait(barrier, len(peers))
+
+
+def front_kernel(
+    dp, far, tok_ref, gain_ref, w1_ref, w2_ref, fac_ref, idr_ref, idc_ref,
+    q_out, k_out, v_out, norm_out, wpad_out, att_out, lse_ref, got_out, wide_out,
+    norm, wpad, qkv, att, got, vt_ref, z1, y1, x2, pair,
+    sx, rx, sc, rc, sf, rf, sz1, rz1, sy1, ry1, sx2, rx2, sz2, rz2, sy2, ry2, sc2, rc2,
+    st_, rt_, so,
+):
+    here, me = lax.axis_index("tensor"), lax.axis_index("dp")
+    rows, width = tok_ref.shape
+    length = norm.shape[0]
+    tiles = length // TILE
+    cols = w1_ref.shape[2] // 2
+    heads = cols // HD
+    packed = w1_ref.shape[1]
+    depth = 2 * packed
+    fused = far > 0
+    major, minor = me // 2, me % 2
+
+    def at(mask):
+        return (me, here ^ mask)
+
+    across = (me ^ 1, here)
+
+    def along(step):
+        return (lax.rem(major + step, far) * 2 + minor, here)
+
+    def source(step):
+        return lax.rem(major + far - step, far)
+
+    peers = [at(mask) for mask in PARTNERS]
+    if fused:
+        peers += [across] + [along(step) for step in range(1, far)]
+    greet(peers)
+
+    def z_first(w, step):
+        return remote(
+            w1_ref.at[w], z1.at[step, w], sz1.at[step, w], rz1.at[step, w], along(step)
+        )
+
+    def y_first(w, step):
+        src = w1_ref.at[w] if isinstance(step, int) and step == 0 else z1.at[step, w]
+        return remote(src, y1.at[step, w], sy1.at[step, w], ry1.at[step, w], across)
+
+    swap_two = remote(w2_ref, x2, sx2, rx2, at(2)) if fused else None
+    if fused:
+        for w in range(3):
+            for step in range(1, far):
+                z_first(w, step).start()
+            y_first(w, 0).start()
+
+    chunk = TILE
+    count = rows // chunk
+
+    @pl.loop(0, count)
+    def _(c):
+        low = pl.multiple_of(c * chunk, chunk)
+        v = tok_ref[pl.ds(low, chunk), :].astype(F32)
+        hat = v * lax.rsqrt(jnp.mean(v * v, axis=-1, keepdims=True) + EPSILON)
+        norm[pl.ds(pl.multiple_of(here * rows + low, chunk), chunk), :] = (
+            hat * gain_ref[...]
+        ).astype(BF)
+
+    def rows_of(mask, c):
+        return norm.at[pl.ds(pl.multiple_of((here ^ mask) * rows + c * chunk, chunk), chunk), :]
+
+    def send_x(c):
+        return remote(rows_of(0, c), rows_of(0, c), sx.at[c], rx.at[c], at(2))
+
+    def send_c(c):
+        return remote(rows_of(0, c), rows_of(0, c), sc.at[c], rc.at[c], at(1))
+
+    def forward(c):
+        return remote(rows_of(2, c), rows_of(2, c), sf.at[c], rf.at[c], at(1))
+
+    for c in range(count):
+        send_x(c).start()
+        send_c(c).start()
+    if fused:
+        swap_two.start()
+
+    def project(w, mask, c):
+        low = pl.multiple_of((here ^ mask) * rows + c * chunk, chunk)
+        y = mm(norm[pl.ds(low, chunk), :], wpad[w], 1, 0)
+        if w == 0:
+            y = y * fac_ref[...]
+        y = y.astype(BF)
+        for h in range(heads):
+            qkv[w, h, pl.ds(low, chunk), :] = y[:, h * HP : (h + 1) * HP]
+
+    if not fused:
+        wpad[...] = w1_ref[...]
+        for c in range(count):
+            send_c(c).wait_recv()
+        for w in range(3):
+            for mask in (0, 1):
+                for c in range(count):
+                    project(w, mask, c)
+    else:
+        wpad[...] = jnp.zeros_like(wpad)
+
+        def unpack(w, block, device):
+            for part in range(2):
+                low = pl.multiple_of(device * depth + part * packed, 16)
+                for h in range(heads):
+                    lane = part * cols + h * HD
+                    wpad[w, pl.ds(low, packed), h * HP : h * HP + HD] = block[:, lane : lane + HD]
+
+        for w in (1, 0, 2):
+            unpack(w, w1_ref[w], me)
+            for step in range(1, far):
+                z_first(w, step).wait_recv()
+                y_first(w, step).start()
+                unpack(w, z1[step, w], source(step) * 2 + minor)
+            for step in range(far):
+                y_first(w, step).wait_recv()
+                unpack(w, y1[step, w], source(step) * 2 + 1 - minor)
+            if w == 1:
+                for c in range(count):
+                    send_c(c).wait_recv()
+            for mask in (0, 1):
+                for c in range(count):
+                    project(w, mask, c)
+
+    def rows_two(index):
+        return pl.ds(pl.multiple_of(index * depth, 16), depth)
+
+    def z_second(w, step):
+        return remote(
+            pair.at[w], wide_out.at[w, rows_two(me), pl.ds(0, 2 * cols)],
+            sz2.at[w, step], rz2.at[w, step], along(step),
+        )
+
+    def block_two(w, index):
+        return wide_out.at[w, rows_two(index), pl.ds(0, 2 * cols)]
+
+    def y_second(w, step):
+        ref = block_two(w, source(step) * 2 + minor)
+        return remote(ref, ref, sy2.at[w, step], ry2.at[w, step], across)
+
+    def c_second(w, step, side):
+        index = source(step) * 2 + (minor if side == 0 else 1 - minor)
+        return remote(
+            block_two(w, index), wide_out.at[w, rows_two(index), pl.ds(2 * cols, 2 * cols)],
+            sc2.at[w, step, side], rc2.at[w, step, side], at(1),
+        )
+
+    def own_two(w):
+        return pltpu.make_async_copy(pair.at[w], block_two(w, me), so.at[8 + w])
+
+    if fused:
+        swap_two.wait_recv()
+        for w in range(3):
+            for which, ref in ((0, w2_ref), (1, x2)):
+                block = ref[w]
+                for part in range(2):
+                    pair[w, part * packed : (part + 1) * packed,
+                         which * cols : (which + 1) * cols] = (
+                        block[:, part * cols : (part + 1) * cols]
+                    )
+            own_two(w).start()
+            for step in range(1, far):
+                z_second(w, step).start()
+
+    for c in range(count):
+        send_x(c).wait_recv()
+        forward(c).start()
+        for w in range(3):
+            project(w, 2, c)
+    for c in range(count):
+        forward(c).wait_recv()
+        for w in range(3):
+            project(w, 3, c)
+
+    keep = [
+        pltpu.make_async_copy(norm, norm_out, so.at[0]),
+        pltpu.make_async_copy(wpad, wpad_out, so.at[1]),
+        pltpu.make_async_copy(qkv.at[0], q_out, so.at[2]),
+        pltpu.make_async_copy(qkv.at[1], k_out, so.at[3]),
+        pltpu.make_async_copy(qkv.at[2], v_out, so.at[4]),
+    ]
+    for copy in keep:
+        copy.start()
+
+    def trade(h, mask):
+        spot = pl.ds(pl.multiple_of((here ^ mask) * rows, HP), rows)
+        return remote(
+            att.at[h, :, spot], got.at[SLOT[mask], h], st_.at[mask, h], rt_.at[mask, h], at(mask)
+        )
+
+    def second_on(w):
+        own_two(w).wait()
+        for step in range(far):
+            if step:
+                z_second(w, step).wait_recv()
+            y_second(w, step).start()
+            c_second(w, step, 0).start()
+
+    sub = lax.broadcasted_iota(jnp.int32, (HP, length), 0)
+
+    @pl.loop(0, heads)
+    def _(h):
+        q_ref, k_ref, v_ref = qkv.at[0, h], qkv.at[1, h], qkv.at[2, h]
+        vt_ref[...] = jnp.where(sub == HD, 1.0, v_ref[...].astype(F32).T).astype(BF)
+
+        def scores(t):
+            seen, low = reach(t, length), t * TILE
+            st = mm(k_ref[:seen, :], q_ref[low : low + TILE, :], 1, 1)
+            visible = idc_ref[low:seen, :] <= idr_ref[:, low : low + TILE]
+            masked = jnp.where(visible, st[low:], MASKED)
+            return jnp.concatenate([st[:low], masked], 0) if low else masked
+
+        st = scores(0)
+        for t in range(tiles):
+            later = scores(t + 1) if t + 1 < tiles else None
+            seen, low = st.shape[0], t * TILE
+            group = jnp.max(st.reshape(seen // 64, 64, TILE), axis=0)
+            highest = jnp.max(group, axis=0, keepdims=True)
+            weights = jnp.exp(st - highest).astype(BF)
+            ot = mm(vt_ref[:, :seen], weights, 1, 0)
+            summed = ot[HD : HD + 1, :]
+            att[h, :, low : low + TILE] = (ot[:HD] * (1.0 / summed)).astype(BF)
+            lse_ref[h, :, low : low + TILE] = highest + jnp.log(summed)
+            st = later
+        for mask in PARTNERS:
+            trade(h, mask).start()
+        if fused:
+
+            @pl.when(h > 0)
+            def _():
+                second_on(h - 1)
+
+    got[0] = att[:, :, pl.ds(pl.multiple_of(here * rows, HP), rows)]
+    keep.append(pltpu.make_async_copy(att, att_out, so.at[5]))
+    keep[-1].start()
+    if fused:
+        for w in range(3):
+            for step in range(far):
+                y_second(w, step).wait_recv()
+                c_second(w, step, 1).start()
+    for h in range(heads):
+        for mask in PARTNERS:
+            trade(h, mask).wait_recv()
+    keep.append(pltpu.make_async_copy(got, got_out, so.at[6]))
+    keep[-1].start()
+
+    for c in range(count):
+        send_x(c).wait_send()
+        send_c(c).wait_send()
+        forward(c).wait_send()
+    for h in range(heads):
+        for mask in PARTNERS:
+            trade(h, mask).wait_send()
+    if fused:
+        swap_two.wait_send()
+        for w in range(3):
+            for step in range(far):
+                if step:
+                    z_first(w, step).wait_send()
+                    z_second(w, step).wait_send()
+                y_first(w, step).wait_send()
+                y_second(w, step).wait_send()
+                c_second(w, step, 0).wait()
+                c_second(w, step, 1).wait()
+    for copy in keep:
+        copy.wait()
+
+
+def front(dp, far, tokens, gain, first, second, factor, idr, idc, cols):
+    rows, width = tokens.shape
+    length = idr.shape[1]
+    heads = cols // HD
+    wide = heads * HP
+    packed = first.shape[1]
+    count = rows // TILE
+    vmem = pl.BlockSpec(memory_space=pltpu.VMEM)
+    hbm = pl.BlockSpec(memory_space=pl.ANY)
+    sem = pltpu.SemaphoreType.DMA
+    far_n = max(far, 1)
+    fused = far > 0
+    small = (packed, 2 * cols) if fused else (16, 128)
+    per_head = jax.ShapeDtypeStruct((heads, length, HP), BF)
+    return pl.pallas_call(
+        lambda *refs: front_kernel(dp, far, *refs),
+        out_shape=[
+            per_head,
+            per_head,
+            per_head,
+            jax.ShapeDtypeStruct((length, width), BF),
+            jax.ShapeDtypeStruct((3, width, wide), BF),
+            jax.ShapeDtypeStruct((heads, HD, length), BF),
+            jax.ShapeDtypeStruct((heads, 1, length), F32),
+            jax.ShapeDtypeStruct((4, heads, HD, rows), BF),
+            jax.ShapeDtypeStruct((3, width, 4 * cols) if fused else (3, 16, 128), BF),
+        ],
+        in_specs=[vmem] * 7,
+        out_specs=[hbm] * 6 + [vmem] + [hbm] * 2,
+        scratch_shapes=[
+            pltpu.VMEM((length, width), BF),
+            pltpu.VMEM((3, width, wide), BF),
+            pltpu.VMEM((3, heads, length, HP), BF),
+            pltpu.VMEM((heads, HD, length), BF),
+            pltpu.VMEM((4, heads, HD, rows), BF),
+            pltpu.VMEM((HP, length), BF),
+            pltpu.VMEM((far_n, 3) + small, BF),
+            pltpu.VMEM((far_n, 3) + small, BF),
+            pltpu.VMEM((3,) + small, BF),
+            pltpu.VMEM((3, 2 * packed, 2 * cols) if fused else (3, 16, 128), BF),
+            sem((count,)), sem((count,)), sem((count,)), sem((count,)), sem((count,)), sem((count,)),
+            sem((far_n, 3)), sem((far_n, 3)), sem((far_n, 3)), sem((far_n, 3)),
+            sem, sem,
+            sem((3, far_n)), sem((3, far_n)), sem((3, far_n)), sem((3, far_n)),
+            sem((3, far_n, 2)), sem((3, far_n, 2)),
+            sem((4, heads)), sem((4, heads)),
+            sem((12,)),
+        ],
+        compiler_params=pltpu.CompilerParams(
+            vmem_limit_bytes=60 << 20, collective_id=1, has_side_effects=True
+        ),
+    )(tokens, gain, first, second, factor, idr, idc)
 
 
 def swap(v, axis, size, mask):
@@ -193,6 +482,11 @@
     return (stack[0] + stack[1]) + (stack[2] + stack[3])
 
 
+def pack(w):
+    half = w.shape[0] // 2
+    return jnp.concatenate([w[:half], w[half:]], axis=1)
+
+
 def pad_heads(w):
     rows, cols = w.shape
     w = w.reshape(rows, cols // HD, HD)
@@ -226,57 +520,34 @@
 
     tokens_f32 = tokens.astype(F32)
     hat_one, inverse_one = rms_stats(tokens_f32)
-    normed_own = (hat_one * attn_gain).astype(BF)
-    normed_x = swap(normed_own, "tensor", tensor, 2)
-    blocks = [normed_own, normed_x, swap(normed_own, "tensor", tensor, 1)]
-    blocks.append(swap(normed_x, "tensor", tensor, 1))
-    normed = jnp.zeros((length, width), BF)
-    for at, block in zip(order, blocks):
-        normed = lax.dynamic_update_slice(normed, block, (at * rows, 0))
-
-    first = jnp.concatenate([w_query, w_key, w_value], axis=1)
-    second = jnp.concatenate([w_out.T, w_up, w_down.T], axis=1)
-    full_qkv = gather_dp(first, dp).reshape(width, 3 * cols)
-    pair = jnp.concatenate([second, swap(second, "tensor", tensor, 2)], axis=1)
-    half = gather_dp(pair, dp).reshape(width, 6 * cols)
-    both = swap(half, "tensor", tensor, 1)
-
-    def wide(at):
-        return jnp.concatenate(
-            [
-                half[:, at * cols : (at + 1) * cols],
-                half[:, (3 + at) * cols : (4 + at) * cols],
-                both[:, at * cols : (at + 1) * cols],
-                both[:, (3 + at) * cols : (4 + at) * cols],
-            ],
-            axis=1,
-        )
-
-    out_t, up, down_t = wide(0), wide(1), wide(2)
-    wq, wk, wv = (pad_heads(full_qkv[:, i * cols : (i + 1) * cols]) for i in range(3))
-
     softplus = jnp.log1p(jnp.exp(query_scale))
     factor = SCORE_BASE / math.sqrt(HD) * softplus
     factor_pad = jnp.pad(factor, (0, HP - HD))[None, :]
-    queries = (mm(normed, wq, 1, 0) * jnp.tile(factor_pad, (1, heads))).astype(BF)
-    keys = mm(normed, wk, 1, 0).astype(BF)
-    values = mm(normed, wv, 1, 0).astype(BF)
     idr = block_ids
     idc = block_ids.reshape(length, 1)
-    attended, lse = attend(queries, keys, values, idr, idc)
-
-    def trade(blocks_of):
-        return [
-            blocks_of(here),
-            swap(blocks_of(order[1]), "tensor", tensor, 2),
-            swap(blocks_of(order[2]), "tensor", tensor, 1),
-            swap(blocks_of(order[3]), "tensor", tensor, 3),
-        ]
-
-    compact = trim_heads(attended)
-    mine = jnp.concatenate(
-        trade(lambda at: lax.dynamic_slice(compact, (at * rows, 0), (rows, cols))), axis=1
+
+    first = (w_query, w_key, w_value)
+    second = (w_out.T, w_up, w_down.T)
+    far = dp // 2 if dp == 8 else 0
+    if far:
+        first = jnp.stack([pack(w) for w in first])
+        second = jnp.stack([pack(w) for w in second])
+    else:
+        pair = [jnp.concatenate([w, swap(w, "tensor", tensor, 2)], axis=1) for w in second]
+        half = gather_dp(jnp.concatenate(pair, axis=1), dp).reshape(width, 3, 2 * cols)
+        both = jnp.concatenate([half, swap(half, "tensor", tensor, 1)], axis=2)
+        full = gather_dp(jnp.concatenate(first, axis=1), dp).reshape(width, 3 * cols)
+        first = jnp.stack([pad_heads(full[:, i * cols : (i + 1) * cols]) for i in range(3)])
+        second = jnp.zeros((3, 16, 128), BF)
+    queries, keys, values, normed, padded, attended, lse, got, wide = front(
+        dp, far, tokens, attn_gain[None, :], first, second, jnp.tile(factor_pad, (1, heads)),
+        idr, idc, cols,
     )
+    if not far:
+        wide = both.transpose(1, 0, 2)
+    wq, wk, wv = padded[0], padded[1], padded[2]
+    out_t, up, down_t = wide[0], wide[1], wide[2]
+    mine = got.reshape(4 * cols, rows).T
     hidden = tokens_f32 + mm(mine, out_t, 1, 1)
 
     b_rel = jnp.concatenate([lax.dynamic_slice(b_up, (at * cols,), (cols,)) for at in order])

time: 608 us -> 518 us (0.85); the launches traced: 598 us -> 515 us
  Pallas kernels: 52.4 us -> 157 us
  local copies, waits for them, and re-layouts: 175 us -> 107 us
  waiting for transfers between devices: 174 us -> 106 us
  starting transfers between devices: 75.6 us -> 30.2 us
  matrix products: 88.5 us -> 68 us
  between operations: 2.09 us -> 13.6 us
    pallas_call x1, Pallas kernels: 20 us -> 124 us  [front(): pl.pallas_call(lambda *refs: front_kernel(dp, far, *refs), out_shape=[per...]
    ppermute x32 -> x16, waiting for transfers between devices: 92.1 us -> 33 us  [swap(): return lax.ppermute(v, axis, [(i, i ^ mask) for i in range(size)])]
    concatenate x4 -> x0, local copies, waits for them, and re-layouts: 33.4 us -> none  [the longest x3 31.4 us: wide(): jnp.concatenate([half[:, at * cols:(at + 1) * cols], half[:, (3 + at) * c...]
    ppermute x6 -> x0, starting transfers between devices: 22.7 us -> none  [gather_dp(): lax.ppermute(shard, 'dp', [(i, (i + 2 * step) % size) for i in range(size)])]
    dot_general x27 -> x24, matrix products: 88.5 us -> 68 us  [mm(): lax.dot_general(a, b, (((ca,), (cb,)), ((), ())), preferred_element_type=...]
    dynamic_update_slice x18 -> x0, local copies, waits for them, and re-layouts: 19.6 us -> none  [the longest x7 8.82 us: gather_dp(): lax.dynamic_update_slice(whole, parts[step][None], (source + minor, 0, 0))]
    ppermute x32 -> x16, starting transfers between devices: 30.3 us -> 11 us  [swap(): return lax.ppermute(v, axis, [(i, i ^ mask) for i in range(size)])]
    slice x6, local copies, waits for them, and re-layouts: 19.3 us -> 5.24 us  [pack(): return jnp.concatenate([w[:half], w[half:]], axis=1)]
  transfers between devices with their start and end apart: 50 -> 28, of which waited for: 21 -> 13; matrix products, arithmetic and copies ran while one was open for 38% -> 31% of each run, Pallas kernels for 9% -> 6%
where the time goes in v2:
time: 518 us; the launch traced here: 515 us
  Pallas kernels  157 us (30%)
  local copies, waits for them, and re-layouts  107 us (21%)
  waiting for transfers between devices  106 us (20%)
  matrix products  68 us (13%)
  other arithmetic  33.2 us (6%)
  starting transfers between devices  30.2 us (6%)
  between operations  13.6 us (3%)
    pallas_call x1, Pallas kernels, front(): pl.pallas_call(lambda *refs: front_kernel(dp, far, *refs), out_shape=[per...  124 us
    dot_general x24, matrix products, mm(): lax.dot_general(a, b, (((ca,), (cb,)), ((), ())), preferred_element_type=...  68 us
    ppermute x6, waiting for transfers between devices, scatter_dp(): lax.ppermute(piece.astype(BF), 'dp', [(i, (i + 2 * step) % size) for i in...  66.3 us
    ppermute x16, waiting for transfers between devices, swap(): return lax.ppermute(v, axis, [(i, i ^ mask) for i in range(size)])  33 us
    pallas_call x1, Pallas kernels, attend_back(): pl.pallas_call(attend_back_kernel, grid=(heads,), out_shape=[jax.ShapeDty...  32.6 us
    concatenate x6, local copies, waits for them, and re-layouts, body(): jnp.concatenate([trim_heads(g) for g in (d_wq, d_wk, d_wv)], axis=1)  31 us
    ppermute x6, starting transfers between devices, sum_all(): lax.ppermute(v, 'dp', [(i, (i + 2 * s) % dp) for i in range(dp)])  11.3 us
    add x1, local copies, waits for them, and re-layouts, body(): keep = keep + swap(give.astype(BF), 'tensor', tensor, 1).astype(F32)  11.1 us
  transfers between devices with their start and end apart: 28, of which 13 were waited for; matrix products, arithmetic and copies ran while one was open for 31% of the time, Pallas kernels for 6%

profile of v2, /device:TPU:0, one launch (start us, length us, event | category | flops | bytes accessed | tf_op | source)
XLA Modules:
  0.0 514.7 jit_solution(15673544619336948724)
XLA Ops:
  13.0 124.1 %shard_map.237 = (bf16[4,2048,128]{2,1,0:T(8,128)(2,1)}, bf16[4,2048,128]{2,1,0:T(8,128)(2,1)}, bf16[4,2048,128]{2,1,0:T(8,128)(2,1)}, bf16[2048,1280]{1,0:T(8,1...) custom-call(bf16[512,1280]{1,0:T(8,128)(2,1)} %refs_0_.1, ...), custom_call_target="tpu_custom_call" | custom-call | tf_op jit(solution)/shard_map/pallas_call | solution.py:390
  137.2 4.4 multiply_reduce_fusion.5
  141.8 4.6 convolution_add_fusion.9
  185.5 6.8 %fusion.27 = bf16[512,1280]{1,0:T(8,128)(2,1)} fusion(f32[512,1280]{1,0:T(8,128)} %copy-done.12, bf16[3,1280,1280]{2,1,0:T(8,128)(2,1)} %get-tuple-element.27, f32[1280]{0:T(1024)S(1)} %copy-done.31, f32[512,1280]{1,0:T(8,128)} %copy-done.33), kind=kOutput, calls=%fused_computation.41 | convolution fusion | flops 1682964480 | bytes 9835520 | tf_op jit(solution)/shard_map/dot_general | solution.py:22
  192.7 3.4 collective-permute-done.23
  205.7 3.5 collective-permute-start.26
  224.1 4.0 copy.95.do_ref
  228.1 32.6 %shard_map.238 = (bf16[2048,512]{1,0:T(8,128)(2,1)}, bf16[2048,512]{1,0:T(8,128)(2,1)}, bf16[2048,512]{1,0:T(8,128)(2,1)}, f32[4,1,128]{2,1,0:T(1,128)}) custom-call(bf16[4,2048,128]{2,1,0:T(8,128)(2,1)} %get-tuple-element.28.q_ref, bf16[4,2048,128]{2,1,0:T(8,128)(2,1)} %get-tuple-element.29.k_ref, bf16[4,2048,128]{2,1,0:T(8,128)(2,1)} %get-tuple-element.30.v_ref, ...), custom_call_target="tpu_custom_call" | custom-call | flops 34359738368 | bytes 16777216 | tf_op jit(solution)/shard_map/pallas_call | solution.py:70
  262.8 7.2 %fusion.129 = f32[1280,512]{0,1:T(8,128)} fusion(bf16[2048,1280]{1,0:T(8,128)(2,1)} %get-tuple-element.37, bf16[2048,512]{1,0:T(8,128)(2,1)S(1)} %copy-done.22), kind=kOutput, calls=%fused_computation.207 | convolution fusion | flops 2684354560 | bytes 9961472 | tf_op jit(solution)/shard_map/dot_general | solution.py:22
  270.0 4.6 fusion.130
  276.2 4.6 fusion.131
  287.5 3.2 copy.86
  290.7 3.3 copy.88
  294.1 5.4 %multiply_reduce_fusion.2 = (f32[1280]{0:T(1024)S(1)}, f32[1280]{0:T(1024)S(1)}, f32[1280]{0:T(1024)S(1)}) fusion(f32[1280,512]{1,0:T(8,128)} %copy.87, bf16[3,1280,512]{2,1,0:T(8,128)(2,1)} %get-tuple-element.34, f32[1280,512]{1,0:T(8,128)} %copy.86, f32[1280,512]{1,0:T(8,128)} %copy.88), kind=kLoop, calls=%fused_computation.61 | loop fusion | flops 5894400 | bytes 11811840 | tf_op jit(solution)/shard_map/reduce_sum | solution.py:619
  315.9 6.1 %concatenate.51 = f32[4,2,160,320]{2,1,0,3:T(2,128)} reshape(f32[1280,4,80]{0,2,1:T(8,128)} %slice.255) | data formatting | bytes 3276800 | tf_op jit(solution)/shard_map/concatenate | solution.py:623
  322.0 4.3 copy.91
  329.0 6.1 %concatenate.50 = f32[4,2,160,320]{2,1,0,3:T(2,128)} reshape(f32[1280,4,80]{0,2,1:T(8,128)} %slice.254) | data formatting | bytes 3276800 | tf_op jit(solution)/shard_map/concatenate | solution.py:623
  335.1 4.3 copy.90
  342.1 6.1 %concatenate.49 = f32[4,2,160,320]{2,1,0,3:T(2,128)} reshape(f32[1280,4,80]{0,2,1:T(8,128)} %slice.253) | data formatting | bytes 3276800 | tf_op jit(solution)/shard_map/concatenate | solution.py:623
  348.2 4.3 copy.89
  353.7 3.9 pad_maximum_fusion
  366.5 6.3 %maximum_add_fusion = f32[1280,1920]{0,1:T(8,128)} fusion(f32[1280,640]{0,1:T(8,128)S(1)} %slice-done.2, f32[1280,640]{0,1:T(8,128)S(1)} %slice-done, f32[1280,640]{0,1:T(8,128)S(1)} %slice-done.1, bf16[1280,1920]{0,1:T(8,128)(2,1)} %collective-permute-done.16), kind=kLoop, calls=%fused_computation | loop fusion | flops 9830400 | bytes 24576000 | tf_op jit(solution)/shard_map/add | solution.py:591
  372.7 11.1 %copy.92 = f32[1280,1920]{1,0:T(8,128)} copy(f32[1280,1920]{0,1:T(8,128)} %maximum_add_fusion) | data formatting | bytes 19660800 | tf_op jit(solution)/shard_map/add | solution.py:591
  387.9 5.5 %collective-permute-done.12 = bf16[4,160,960]{2,1,0:T(8,128)(2,1)} collective-permute-done((bf16[4,160,960]{2,1,0:T(8,128)(2,1)}, bf16[4,160,960]{2,1,0:T(8,128)(2,1)}, u32[]{:S(2)}, u32[]{:S(2)}) %collective-permute-start.12) | collective-permute-done | bytes 1228832 | tf_op jit(solution)/shard_map/ppermute | solution.py:431
  402.5 5.0 collective-permute-done.15
  407.6 16.1 %collective-permute-done.14 = bf16[160,960]{1,0:T(8,128)(2,1)S(1)} collective-permute-done((bf16[160,960]{1,0:T(8,128)(2,1)S(1)}, bf16[160,960]{1,0:T(8,128)(2,1)S(1)}, u32[]{:S(2)}, u32[]{:S(2)}) %collective-permute-start.14) | collective-permute-done | bytes 307232 | tf_op jit(solution)/shard_map/ppermute | solution.py:465
  424.8 19.2 %collective-permute-done.17 = bf16[4,160,1920]{2,1,0:T(8,128)(2,1)S(1)} collective-permute-done((bf16[4,160,1920]{2,1,0:T(8,128)(2,1)S(1)}, bf16[4,160,1920]{2,1,0:T(8,128)(2,1)S(1)}, u32[]{:S(2)}, u32[]{:S(2)}) %collective-permute-start.17) | collective-permute-done | bytes 2457632 | tf_op jit(solution)/shard_map/ppermute | solution.py:431
  444.6 3.3 collective-permute-start.20
  448.8 4.6 fusion.38
  453.4 8.9 %collective-permute-done.20 = bf16[160,1920]{1,0:T(8,128)(2,1)S(1)} collective-permute-done((bf16[160,1920]{1,0:T(8,128)(2,1)S(1)}, bf16[160,1920]{1,0:T(8,128)(2,1)S(1)}, u32[]{:S(2)}, u32[]{:S(2)}) %collective-permute-start.20) | collective-permute-done | bytes 614432 | tf_op jit(solution)/shard_map/ppermute | solution.py:465
  462.3 36.3 %collective-permute-done.19 = bf16[160,1920]{1,0:T(8,128)(2,1)S(1)} collective-permute-done((bf16[160,1920]{1,0:T(8,128)(2,1)S(1)}, bf16[160,1920]{1,0:T(8,128)(2,1)S(1)}, u32[]{:S(2)}, u32[]{:S(2)}) %collective-permute-start.19) | collective-permute-done | bytes 614432 | tf_op jit(solution)/shard_map/ppermute | solution.py:465
  506.1 4.7 fusion.42
  (240 shorter events, 133.5 us)
Async XLA Ops:
  10.6 126.5 %copy-start.6 = (bf16[512,1280]{1,0:T(8,128)(2,1)S(1)}, bf16[512,1280]{1,0:T(8,128)(2,1)}, u32[]{:S(2)}) copy-start(bf16[512,1280]{1,0:T(8,128)(2,1)} %refs_0_.1) | copy-start | bytes 3932164
  158.0 57.4 %collective-permute-start = (bf16[512,320]{1,0:T(8,128)(2,1)}, bf16[512,320]{1,0:T(8,128)(2,1)}, u32[]{:S(2)}, u32[]{:S(2)}) collective-permute-start(bf16[512,320]{1,0:T(8,128)(2,1)} %get-tuple-element.74), channel_id=1, source_target_pairs={{0,2},{1,3},{2,0},{3,1},{4,6},{5,7},{6,4},{7,5},{8,10},{9,11},{10,... | collective-permute-start | bytes 983048 | tf_op jit(solution)/shard_map/ppermute | solution.py:431
  158.0 58.6 %collective-permute-start.1 = (bf16[512,320]{1,0:T(8,128)(2,1)}, bf16[512,320]{1,0:T(8,128)(2,1)}, u32[]{:S(2)}, u32[]{:S(2)}) collective-permute-start(bf16[512,320]{1,0:T(8,128)(2,1)} %get-tuple-element.73), channel_id=1, source_target_pairs={{0,1},{1,0},{2,3},{3,2},{4,5},{5,4},{6,7},{7,6},{8,9},{9,8},{10,11... | collective-permute-start | bytes 983048 | tf_op jit(solution)/shard_map/ppermute | solution.py:431
  158.4 60.9 %collective-permute-start.2 = (bf16[512,320]{1,0:T(8,128)(2,1)}, bf16[512,320]{1,0:T(8,128)(2,1)}, u32[]{:S(2)}, u32[]{:S(2)}) collective-permute-start(bf16[512,320]{1,0:T(8,128)(2,1)} %get-tuple-element.72), channel_id=1, source_target_pairs={{0,3},{1,2},{2,1},{3,0},{4,7},{5,6},{6,5},{7,4},{8,11},{9,10},{10,... | collective-permute-start | bytes 983048 | tf_op jit(solution)/shard_map/ppermute | solution.py:431
  183.8 181.4 %collective-permute-start.16 = (bf16[1280,1920]{0,1:T(8,128)(2,1)}, bf16[1280,1920]{0,1:T(8,128)(2,1)}, u32[]{:S(2)}, u32[]{:S(2)}) collective-permute-start(bf16[1280,1920]{0,1:T(8,128)(2,1)} %pad_maximum_fusion.1), channel_id=1, source_target_pairs={{0,1},{1,0},{2,3},{3,2},{4,5},{5,4},{6,7},{7,6},{8,9},{9,8},{10,11... | collective-permute-start | bytes 14745608 | tf_op jit(solution)/shard_map/ppermute | solution.py:431
  184.9 7.3 %collective-permute-start.22 = (f32[3,1280]{1,0:T(4,128)S(1)}, f32[3,1280]{1,0:T(4,128)S(1)}, u32[]{:S(2)}, u32[]{:S(2)}) collective-permute-start(f32[3,1280]{1,0:T(4,128)S(1)} %pad_maximum_fusion.4), channel_id=1, source_target_pairs={{0,1},{1,0},{2,3},{3,2},{4,5},{5,4},{6,7},{7,6},{8,9},{9,8},{10,11... | collective-permute-start | bytes 46088 | tf_op jit(solution)/shard_map/ppermute | solution.py:431
  192.3 3.8 collective-permute-start.23
  196.2 3.8 collective-permute-start.24
  200.0 5.6 %collective-permute-start.25 = (f32[3,1280]{1,0:T(4,128)S(1)}, f32[3,1280]{1,0:T(4,128)S(1)}, u32[]{:S(2)}, u32[]{:S(2)}) collective-permute-start(f32[3,1280]{1,0:T(4,128)S(1)} %get-tuple-element.61), channel_id=1, source_target_pairs={{0,8},{4,12},{8,16},{12,20},{16,24},{20,28},{24,0},{28,4},{1,9},{5... | collective-permute-start | bytes 46088 | tf_op jit(solution)/shard_map/ppermute | solution.py:477
  205.7 5.3 %collective-permute-start.26 = (f32[3,1280]{1,0:T(4,128)S(1)}, f32[3,1280]{1,0:T(4,128)S(1)}, u32[]{:S(2)}, u32[]{:S(2)}) collective-permute-start(f32[3,1280]{1,0:T(4,128)S(1)} %get-tuple-element.61), channel_id=1, source_target_pairs={{0,16},{4,20},{8,24},{12,28},{16,0},{20,4},{24,8},{28,12},{1,17},{... | collective-permute-start | bytes 46088 | tf_op jit(solution)/shard_map/ppermute | solution.py:477
  210.9 3.8 collective-permute-start.27
  228.1 32.6 %copy-start = (bf16[3,1280,512]{2,1,0:T(8,128)(2,1)S(1)}, bf16[3,1280,512]{2,1,0:T(8,128)(2,1)}, u32[]{:S(2)}) copy-start(bf16[3,1280,512]{2,1,0:T(8,128)(2,1)} %get-tuple-element.34) | copy-start | bytes 11796484
  282.8 116.6 %collective-permute-start.4 = (bf16[512,1280]{1,0:T(8,128)(2,1)}, bf16[512,1280]{1,0:T(8,128)(2,1)}, u32[]{:S(2)}, u32[]{:S(2)}) collective-permute-start(bf16[512,1280]{1,0:T(8,128)(2,1)} %fusion.31), channel_id=1, source_target_pairs={{0,2},{1,3},{2,0},{3,1},{4,6},{5,7},{6,4},{7,5},{8,10},{9,11},{10,... | collective-permute-start | bytes 3932168 | tf_op jit(solution)/shard_map/ppermute | solution.py:431
  299.6 11.0 %collective-permute-start.6 = (f32[11,128]{1,0:T(8,128)S(1)}, f32[11,128]{1,0:T(8,128)S(1)}, u32[]{:S(2)}, u32[]{:S(2)}) collective-permute-start(f32[11,128]{1,0:T(8,128)S(1)} %fusion.115), channel_id=1, source_target_pairs={{0,1},{1,0},{2,3},{3,2},{4,5},{5,4},{6,7},{7,6},{8,9},{9,8},{10,11... | collective-permute-start | bytes 16904 | tf_op jit(solution)/shard_map/ppermute | solution.py:431
  310.0 138.7 %collective-permute-start.3 = (bf16[512,1280]{1,0:T(8,128)(2,1)}, bf16[512,1280]{1,0:T(8,128)(2,1)}, u32[]{:S(2)}, u32[]{:S(2)}) collective-permute-start(bf16[512,1280]{1,0:T(8,128)(2,1)} %fusion.30), channel_id=1, source_target_pairs={{0,2},{1,3},{2,0},{3,1},{4,6},{5,7},{6,4},{7,5},{8,10},{9,11},{10,... | collective-permute-start | bytes 3932168 | tf_op jit(solution)/shard_map/ppermute | solution.py:431
  310.6 41.8 %collective-permute-start.7 = (f32[11,128]{1,0:T(8,128)S(1)}, f32[11,128]{1,0:T(8,128)S(1)}, u32[]{:S(2)}, u32[]{:S(2)}) collective-permute-start(f32[11,128]{1,0:T(8,128)S(1)} %fusion.146), channel_id=1, source_target_pairs={{0,2},{1,3},{2,0},{3,1},{4,6},{5,7},{6,4},{7,5},{8,10},{9,11},{10,... | collective-permute-start | bytes 16904 | tf_op jit(solution)/shard_map/ppermute | solution.py:431
  352.5 5.1 collective-permute-start.8
  357.6 5.5 %collective-permute-start.9 = (f32[11,128]{1,0:T(8,128)S(1)}, f32[11,128]{1,0:T(8,128)S(1)}, u32[]{:S(2)}, u32[]{:S(2)}) collective-permute-start(f32[11,128]{1,0:T(8,128)S(1)} %get-tuple-element.63), channel_id=1, source_target_pairs={{0,8},{4,12},{8,16},{12,20},{16,24},{20,28},{24,0},{28,4},{1,9},{5... | collective-permute-start | bytes 16904 | tf_op jit(solution)/shard_map/ppermute | solution.py:477
  361.4 32.0 %collective-permute-start.12 = (bf16[4,160,960]{2,1,0:T(8,128)(2,1)}, bf16[4,160,960]{2,1,0:T(8,128)(2,1)}, u32[]{:S(2)}, u32[]{:S(2)}) collective-permute-start(bf16[4,160,960]{2,1,0:T(8,128)(2,1)} %fusion.45), channel_id=1, source_target_pairs={{0,4},{4,0},{8,12},{12,8},{16,20},{20,16},{24,28},{28,24},{1,5},{5... | collective-permute-start | bytes 3686408 | tf_op jit(solution)/shard_map/ppermute | solution.py:431
  363.1 23.5 %collective-permute-start.10 = (f32[11,128]{1,0:T(8,128)S(1)}, f32[11,128]{1,0:T(8,128)S(1)}, u32[]{:S(2)}, u32[]{:S(2)}) collective-permute-start(f32[11,128]{1,0:T(8,128)S(1)} %get-tuple-element.63), channel_id=1, source_target_pairs={{0,16},{4,20},{8,24},{12,28},{16,0},{20,4},{24,8},{28,12},{1,17},{... | collective-permute-start | bytes 16904 | tf_op jit(solution)/shard_map/ppermute | solution.py:477
  365.2 21.6 %collective-permute-start.11 = (f32[11,128]{1,0:T(8,128)S(1)}, f32[11,128]{1,0:T(8,128)S(1)}, u32[]{:S(2)}, u32[]{:S(2)}) collective-permute-start(f32[11,128]{1,0:T(8,128)S(1)} %get-tuple-element.63), channel_id=1, source_target_pairs={{0,24},{4,28},{8,0},{12,4},{16,8},{20,12},{24,16},{28,20},{1,25},{... | collective-permute-start | bytes 16904 | tf_op jit(solution)/shard_map/ppermute | solution.py:477
  383.8 16.3 %copy-start.21 = (bf16[2048,512]{1,0:T(8,128)(2,1)S(1)}, bf16[2048,512]{1,0:T(8,128)(2,1)}, u32[]{:S(2)}) copy-start(bf16[2048,512]{1,0:T(8,128)(2,1)} %get-tuple-element.36) | copy-start | bytes 6291460
  386.6 57.4 %collective-permute-start.17 = (bf16[4,160,1920]{2,1,0:T(8,128)(2,1)S(1)}, bf16[4,160,1920]{2,1,0:T(8,128)(2,1)S(1)}, u32[]{:S(2)}, u32[]{:S(2)}) collective-permute-start(bf16[4,160,1920]{2,1,0:T(8,128)(2,1)S(1)} %fusion.44), channel_id=1, source_target_pairs={{0,4},{4,0},{8,12},{12,8},{16,20},{20,16},{24,28},{28,24},{1,5},{5... | collective-permute-start | bytes 7372808 | tf_op jit(solution)/shard_map/ppermute | solution.py:431
  396.3 11.3 %collective-permute-start.15 = (bf16[160,960]{1,0:T(8,128)(2,1)S(1)}, bf16[160,960]{1,0:T(8,128)(2,1)S(1)}, u32[]{:S(2)}, u32[]{:S(2)}) collective-permute-start(bf16[160,960]{1,0:T(8,128)(2,1)S(1)} %get-tuple-element.68), channel_id=1, source_target_pairs={{0,24},{4,28},{8,0},{12,4},{16,8},{20,12},{24,16},{28,20},{1,25},{... | collective-permute-start | bytes 921608 | tf_op jit(solution)/shard_map/ppermute | solution.py:465
  399.4 24.3 %collective-permute-start.14 = (bf16[160,960]{1,0:T(8,128)(2,1)S(1)}, bf16[160,960]{1,0:T(8,128)(2,1)S(1)}, u32[]{:S(2)}, u32[]{:S(2)}) collective-permute-start(bf16[160,960]{1,0:T(8,128)(2,1)S(1)} %get-tuple-element.69), channel_id=1, source_target_pairs={{0,16},{4,20},{8,24},{12,28},{16,0},{20,4},{24,8},{28,12},{1,17},{... | collective-permute-start | bytes 921608 | tf_op jit(solution)/shard_map/ppermute | solution.py:465
  399.4 24.3 %collective-permute-start.13 = (bf16[160,960]{1,0:T(8,128)(2,1)S(1)}, bf16[160,960]{1,0:T(8,128)(2,1)S(1)}, u32[]{:S(2)}, u32[]{:S(2)}) collective-permute-start(bf16[160,960]{1,0:T(8,128)(2,1)S(1)} %get-tuple-element.67), channel_id=1, source_target_pairs={{0,8},{4,12},{8,16},{12,20},{16,24},{20,28},{24,0},{28,4},{1,9},{5... | collective-permute-start | bytes 921608 | tf_op jit(solution)/shard_map/ppermute | solution.py:465
  400.1 43.9 %copy-start.3 = (f32[1280,1920]{1,0:T(8,128)S(1)}, f32[1280,1920]{1,0:T(8,128)}, u32[]{:S(2)}) copy-start(f32[1280,1920]{1,0:T(8,128)} %copy.92) | copy-start | bytes 29491204
  407.5 41.2 %collective-permute-start.5 = (bf16[512,1280]{1,0:T(8,128)(2,1)S(1)}, bf16[512,1280]{1,0:T(8,128)(2,1)S(1)}, u32[]{:S(2)}, u32[]{:S(2)}) collective-permute-start(bf16[512,1280]{1,0:T(8,128)(2,1)S(1)} %add_convert_fusion), channel_id=1, source_target_pairs={{0,1},{1,0},{2,3},{3,2},{4,5},{5,4},{6,7},{7,6},{8,9},{9,8},{10,11... | collective-permute-start | bytes 3932168 | tf_op jit(solution)/shard_map/ppermute | solution.py:431
  444.6 17.7 %collective-permute-start.20 = (bf16[160,1920]{1,0:T(8,128)(2,1)S(1)}, bf16[160,1920]{1,0:T(8,128)(2,1)S(1)}, u32[]{:S(2)}, u32[]{:S(2)}) collective-permute-start(bf16[160,1920]{1,0:T(8,128)(2,1)S(1)} %get-tuple-element.65), channel_id=1, source_target_pairs={{0,24},{4,28},{8,0},{12,4},{16,8},{20,12},{24,16},{28,20},{1,25},{... | collective-permute-start | bytes 1843208 | tf_op jit(solution)/shard_map/ppermute | solution.py:465
  447.9 50.6 %collective-permute-start.19 = (bf16[160,1920]{1,0:T(8,128)(2,1)S(1)}, bf16[160,1920]{1,0:T(8,128)(2,1)S(1)}, u32[]{:S(2)}, u32[]{:S(2)}) collective-permute-start(bf16[160,1920]{1,0:T(8,128)(2,1)S(1)} %get-tuple-element.66), channel_id=1, source_target_pairs={{0,16},{4,20},{8,24},{12,28},{16,0},{20,4},{24,8},{28,12},{1,17},{... | collective-permute-start | bytes 1843208 | tf_op jit(solution)/shard_map/ppermute | solution.py:465
  447.9 50.6 %collective-permute-start.18 = (bf16[160,1920]{1,0:T(8,128)(2,1)S(1)}, bf16[160,1920]{1,0:T(8,128)(2,1)S(1)}, u32[]{:S(2)}, u32[]{:S(2)}) collective-permute-start(bf16[160,1920]{1,0:T(8,128)(2,1)S(1)} %get-tuple-element.64), channel_id=1, source_target_pairs={{0,8},{4,12},{8,16},{12,20},{16,24},{20,28},{24,0},{28,4},{1,9},{5... | collective-permute-start | bytes 1843208 | tf_op jit(solution)/shard_map/ppermute | solution.py:465
  505.5 8.1 %collective-permute-start.21 = (bf16[160,3,320]{2,0,1:T(8,128)(2,1)S(1)}, bf16[160,3,320]{2,0,1:T(8,128)(2,1)S(1)}, u32[]{:S(2)}, u32[]{:S(2)}) collective-permute-start(bf16[160,3,320]{2,0,1:T(8,128)(2,1)S(1)} %bitcast.201), channel_id=1, source_target_pairs={{0,2},{1,3},{2,0},{3,1},{4,6},{5,7},{6,4},{7,5},{8,10},{9,11},{10,... | collective-permute-start | bytes 921608 | tf_op jit(solution)/shard_map/ppermute | solution.py:431
  (36 other events, 215.3 us)
